TPU v7x, 128 devices: a whole 4x4x4 slice. The times are simulated.
128 devices in a mesh: row: 8 (over z_lo, x), col: 16 (over y, z_hi, core).
Axes of the slice: x: 4, y: 4, z: 4 (z_hi: 2, z_lo: 2; z = z_hi * 2 + z_lo), core: 2. Of those that a mesh axis runs over, the one named last changes fastest.
Arguments:
- features: bfloat16 [16, 256, 64, 1024], P('row', 'col'), may hold values from -6 to 6
- tissue: int32 [16, 256, 64], P('row', 'col'), may hold values 0 or 1
- probe: float32 [16, 256, 4096], P('row', 'col'), may hold values from -6 to 6
Outputs:
- basis: float32 [16, 256, 4096], P('row', 'col')
All inputs are finite; a program needn't handle non-finite values. No bound on the sum of `tissue` on one device may be relied on, other than what follows from the above.
Results may differ from a plain program's by a relative error of at most 0.00091.
Values may be sent and summed in bfloat16 or wider, within the bound.
A program may use at most 128 MiB of HBM per device.

v0:
```python
import functools
import math

import jax
import jax.numpy as jnp
from jax import lax
from jax.sharding import Mesh
from jax.sharding import PartitionSpec as P

RANK = 64
ITERS = 3
ROW = ("row_0", "row_1")
COL = ("col_0", "col_1", "col_2")
ROW_COL = ("row_0", "row_1", "col_0", "col_1", "col_2")


AFFINITY_TEMP = 4.0


def with_halo(shard, sides, width):
    for axis, dim in sides:
        count, length = (lax.axis_size(axis), shard.shape[dim])
        up = [(i, (i + 1) % count) for i in range(count - 1)]
        down = [(j, i) for i, j in up]
        last = lax.slice_in_dim(shard, length - width, length, axis=dim)
        leading = lax.slice_in_dim(shard, 0, width, axis=dim)
        before = lax.ppermute(last, axis, up)
        after = lax.ppermute(leading, axis, down)
        shard = jnp.concatenate([before, shard, after], axis=dim)
    return shard


def by_axis(shard, axes):
    return functools.reduce(lax.psum, axes, shard)


def normalized(features):
    values = features.astype(jnp.float32)
    scaled = values * lax.rsqrt(jnp.sum(values * values, axis=-1, keepdims=True) + 1e-06)
    return scaled.astype(jnp.bfloat16)


def tissue_of(masked_unit):
    values = masked_unit.astype(jnp.float32)
    return (jnp.sum(values * values, axis=-1) > 0.5).astype(jnp.float32)


def pair_weights(left_unit, leftward_mask, right_unit, rightward_mask):
    affinity_scores = jnp.einsum(
        "abpd,abqd->abpq", left_unit, right_unit, preferred_element_type=jnp.float32
    )
    return (
        leftward_mask[..., :, None]
        * rightward_mask[..., None, :]
        * jnp.exp(AFFINITY_TEMP * (affinity_scores - 1.0))
    )


def halo_affinity(masked_unit, central_mask):
    first = with_halo(masked_unit, ((ROW, 0),), 1)
    wide_unit = with_halo(first, ((COL, 1),), 1)
    wide_mask = tissue_of(wide_unit)
    tile_rows, tile_cols = (masked_unit.shape[0], masked_unit.shape[1])
    blocks = []
    for shift_row in range(3):
        for shift_col in range(3):
            other = wide_unit[shift_row : shift_row + tile_rows, shift_col : shift_col + tile_cols]
            neighbour_mask = wide_mask[
                shift_row : shift_row + tile_rows, shift_col : shift_col + tile_cols
            ]
            blocks.append(pair_weights(masked_unit, central_mask, other, neighbour_mask))
    return jnp.concatenate(blocks, axis=3)


def panel_context(carried):
    return with_halo(carried, ((ROW, 0), (COL, 1)), 1)


def local(features, tissue, probe):
    tile_rows, tile_cols, patches, width = features.shape
    unit = normalized(features)
    masked_unit = unit * tissue.astype(jnp.bfloat16)[..., None]
    central_mask = tissue.astype(jnp.float32)
    affinity = halo_affinity(masked_unit, central_mask)
    degree = 1.0 + jnp.sum(affinity, axis=-1)
    inverse_root = lax.rsqrt(degree)
    panel = probe.reshape(tile_rows, tile_cols, patches, RANK)
    for step in range(ITERS):
        carried = (inverse_root[..., None] * panel).reshape(tile_rows, tile_cols, patches * RANK)
        own_block = affinity[:, :, :, 4 * patches : 5 * patches]
        summed = jnp.einsum(
            "abpq,abqk->abpk",
            own_block,
            carried.reshape(tile_rows, tile_cols, patches, RANK),
            precision=lax.Precision.HIGHEST,
        )
        wide_panel = panel_context(carried)
        for shift_row in range(3):
            for shift_col in range(3):
                if shift_row != 1 or shift_col != 1:
                    which = 3 * shift_row + shift_col
                    block = affinity[:, :, :, which * patches : (which + 1) * patches]
                    source = wide_panel[
                        shift_row : shift_row + tile_rows, shift_col : shift_col + tile_cols
                    ]
                    source = source.reshape(tile_rows, tile_cols, patches, RANK)
                    summed = summed + jnp.einsum(
                        "abpq,abqk->abpk", block, source, precision=lax.Precision.HIGHEST
                    )
        image = panel + inverse_root[..., None] * summed
        flat = image.reshape(-1, RANK)
        local_gram = jnp.dot(
            flat.T, flat, precision=lax.Precision.HIGHEST, preferred_element_type=jnp.float32
        )
        gram_matrix = by_axis(local_gram, ROW_COL)
        lower = jnp.linalg.cholesky(gram_matrix)
        solved = jax.scipy.linalg.solve_triangular(lower, flat.T, lower=True)
        panel = solved.T.reshape(tile_rows, tile_cols, patches, RANK)
    total = tile_rows * lax.axis_size(ROW) * tile_cols * lax.axis_size(COL) * patches
    factor = math.sqrt(float(total))
    return (factor * panel).reshape(tile_rows, tile_cols, patches * RANK)


def solution(mesh):
    torus = Mesh(mesh.devices.reshape(2, 4, 4, 2, 2), ("row_0", "row_1", "col_0", "col_1", "col_2"))
    return jax.shard_map(
        local,
        mesh=torus,
        in_specs=(P(ROW, COL, None, None), P(ROW, COL, None), P(ROW, COL, None)),
        out_specs=P(ROW, COL, None),
        check_vma=False,
    )
```

profile of v0, /device:TPU:0, one launch (start us, length us, event | category | flops | bytes accessed | tf_op | source)
XLA Modules:
  0.0 580.6 jit_solution(8370487105094242923)
XLA Ops:
  10.4 43.3 %collective-permute-done = bf16[1,16,64,1024]{3,2,1,0:T(8,128)(2,1)S(1)} collective-permute-done((bf16[1,16,64,1024]{3,2,1,0:T(8,128)(2,1)S(1)}, bf16[1,16,64,1024]{3,2,1,0:T(8,128)(2,1)S(1)}, u32[]{:S(2)}, u32[]{:S(2)}) %collective-permute-start) | collective-permute-done | bytes 2097184 | tf_op jit(solution)/shard_map/ppermute | solution.py:27
  63.5 5.3 collective-permute-done.3
  68.8 5.1 multiply_reduce_fusion
  76.2 7.2 %maximum_maximum_fusion = (bf16[4,17,64,1024]{3,2,1,0:T(8,128)(2,1)}, bf16[4,17,64,1024]{3,2,1,0:T(8,128)(2,1)S(1)}) fusion(bf16[1,16,64,1024]{3,2,1,0:T(8,128)(2,1)S(1)} %collective-permute-done.1, bf16[2,16,64,1024]{3,2,1,0:T(8,128)(2,1)S(1)} %copy-done.1, bf16[1,16,64,1024]{3,2,1,0:T(8,128)(2,1)S(1)} %copy-done.3, ...), kind=kLoop, calls=%fused_computation.3 | loop fusion | flops 26738688 | bytes 27262976 | tf_op jit(solution)/shard_map/concatenate | solution.py:29
  113.9 5.7 collective-permute-start.4
  129.3 10.0 %collective-permute-start.6 = (f32[4,1,4096]{2,1,0:T(1,128)}, f32[4,1,4096]{2,1,0:T(1,128)S(1)}, u32[]{:S(2)}, u32[]{:S(2)}) collective-permute-start(f32[4,1,4096]{2,1,0:T(1,128)} %get-tuple-element.45), channel_id=1, source_target_pairs={{0,1},{1,2},{2,3},{3,4},{4,5},{5,6},{6,7},{7,8},{8,9},{9,10},{10,1... | collective-permute-start | bytes 196616 | tf_op jit(solution)/shard_map/ppermute | solution.py:27
  183.8 10.7 %psum.105 = f32[64,64]{0,1:T(8,128)S(1)} all-reduce(f32[64,64]{0,1:T(8,128)S(1)} %convolution_bitcast_fusion.4), channel_id=1, replica_groups=mesh['row_0'=2,'row_1'=4,'col_0'=4,'col_1'=2,'col_2'=2] {'row_0'}, use_global_device_ids=true, to_apply=%region_11.12 | all-reduce | flops 4096 | bytes 32768 | tf_op jit(solution)/shard_map/psum | solution.py:34
  194.5 16.7 %psum.106 = f32[64,64]{0,1:T(8,128)S(1)} all-reduce(f32[64,64]{0,1:T(8,128)S(1)} %psum.105), channel_id=1, replica_groups=mesh['row_0'=2,'row_1'=4,'col_0'=4,'col_1'=2,'col_2'=2] {'row_1'}, use_global_device_ids=true, to_apply=%region_12.13 | all-reduce | flops 4096 | bytes 32768 | tf_op jit(solution)/shard_map/psum | solution.py:34
  211.2 19.7 %psum.107 = f32[64,64]{0,1:T(8,128)S(1)} all-reduce(f32[64,64]{0,1:T(8,128)S(1)} %psum.106), channel_id=1, replica_groups=mesh['row_0'=2,'row_1'=4,'col_0'=4,'col_1'=2,'col_2'=2] {'col_0'}, use_global_device_ids=true, to_apply=%region_13.14 | all-reduce | flops 4096 | bytes 32768 | tf_op jit(solution)/shard_map/psum | solution.py:34
  231.0 12.4 %psum.108 = f32[64,64]{0,1:T(8,128)S(1)} all-reduce(f32[64,64]{0,1:T(8,128)S(1)} %psum.107), channel_id=1, replica_groups=mesh['row_0'=2,'row_1'=4,'col_0'=4,'col_1'=2,'col_2'=2] {'col_1'}, use_global_device_ids=true, to_apply=%region_14.15 | all-reduce | flops 4096 | bytes 32768 | tf_op jit(solution)/shard_map/psum | solution.py:34
  246.9 5.8 %cholesky.59 = f32[64,64]{1,0:T(8,128)S(1)} custom-call(f32[64,64]{1,0:T(8,128)S(1)} %fusion.135), custom_call_target="Cholesky" | custom-call | tf_op jit(solution)/shard_map/jit(cholesky)/cholesky | solution.py:116
  254.1 4.9 custom-call.7
  347.5 11.1 %psum.110 = f32[64,64]{0,1:T(8,128)S(1)} all-reduce(f32[64,64]{0,1:T(8,128)S(1)} %convolution_bitcast_fusion.3), channel_id=1, replica_groups=mesh['row_0'=2,'row_1'=4,'col_0'=4,'col_1'=2,'col_2'=2] {'row_0'}, use_global_device_ids=true, to_apply=%region_18.21 | all-reduce | flops 4096 | bytes 32768 | tf_op jit(solution)/shard_map/psum | solution.py:34
  358.6 14.4 %psum.111 = f32[64,64]{0,1:T(8,128)S(1)} all-reduce(f32[64,64]{0,1:T(8,128)S(1)} %psum.110), channel_id=1, replica_groups=mesh['row_0'=2,'row_1'=4,'col_0'=4,'col_1'=2,'col_2'=2] {'row_1'}, use_global_device_ids=true, to_apply=%region_19.22 | all-reduce | flops 4096 | bytes 32768 | tf_op jit(solution)/shard_map/psum | solution.py:34
  373.0 20.5 %psum.112 = f32[64,64]{0,1:T(8,128)S(1)} all-reduce(f32[64,64]{0,1:T(8,128)S(1)} %psum.111), channel_id=1, replica_groups=mesh['row_0'=2,'row_1'=4,'col_0'=4,'col_1'=2,'col_2'=2] {'col_0'}, use_global_device_ids=true, to_apply=%region_20.23 | all-reduce | flops 4096 | bytes 32768 | tf_op jit(solution)/shard_map/psum | solution.py:34
  393.5 8.4 %psum.113 = f32[64,64]{0,1:T(8,128)S(1)} all-reduce(f32[64,64]{0,1:T(8,128)S(1)} %psum.112), channel_id=1, replica_groups=mesh['row_0'=2,'row_1'=4,'col_0'=4,'col_1'=2,'col_2'=2] {'col_1'}, use_global_device_ids=true, to_apply=%region_21.24 | all-reduce | flops 4096 | bytes 32768 | tf_op jit(solution)/shard_map/psum | solution.py:34
  405.5 5.8 %cholesky.70 = f32[64,64]{1,0:T(8,128)S(1)} custom-call(f32[64,64]{1,0:T(8,128)S(1)} %fusion.133), custom_call_target="Cholesky" | custom-call | tf_op jit(solution)/shard_map/jit(cholesky)/cholesky | solution.py:116
  412.7 4.9 custom-call.8
  503.9 12.7 %psum.115 = f32[64,64]{0,1:T(8,128)S(1)} all-reduce(f32[64,64]{0,1:T(8,128)S(1)} %convolution_bitcast_fusion.2), channel_id=1, replica_groups=mesh['row_0'=2,'row_1'=4,'col_0'=4,'col_1'=2,'col_2'=2] {'row_0'}, use_global_device_ids=true, to_apply=%region_23.26 | all-reduce | flops 4096 | bytes 32768 | tf_op jit(solution)/shard_map/psum | solution.py:34
  516.6 14.4 %psum.116 = f32[64,64]{0,1:T(8,128)S(1)} all-reduce(f32[64,64]{0,1:T(8,128)S(1)} %psum.115), channel_id=1, replica_groups=mesh['row_0'=2,'row_1'=4,'col_0'=4,'col_1'=2,'col_2'=2] {'row_1'}, use_global_device_ids=true, to_apply=%region_24.27 | all-reduce | flops 4096 | bytes 32768 | tf_op jit(solution)/shard_map/psum | solution.py:34
  531.0 20.5 %psum.117 = f32[64,64]{0,1:T(8,128)S(1)} all-reduce(f32[64,64]{0,1:T(8,128)S(1)} %psum.116), channel_id=1, replica_groups=mesh['row_0'=2,'row_1'=4,'col_0'=4,'col_1'=2,'col_2'=2] {'col_0'}, use_global_device_ids=true, to_apply=%region_25.28 | all-reduce | flops 4096 | bytes 32768 | tf_op jit(solution)/shard_map/psum | solution.py:34
  551.5 10.2 %psum.118 = f32[64,64]{0,1:T(8,128)S(1)} all-reduce(f32[64,64]{0,1:T(8,128)S(1)} %psum.117), channel_id=1, replica_groups=mesh['row_0'=2,'row_1'=4,'col_0'=4,'col_1'=2,'col_2'=2] {'col_1'}, use_global_device_ids=true, to_apply=%region_26.29 | all-reduce | flops 4096 | bytes 32768 | tf_op jit(solution)/shard_map/psum | solution.py:34
  565.4 5.8 %cholesky.81 = f32[64,64]{1,0:T(8,128)S(1)} custom-call(f32[64,64]{1,0:T(8,128)S(1)} %fusion.131), custom_call_target="Cholesky" | custom-call | tf_op jit(solution)/shard_map/jit(cholesky)/cholesky | solution.py:116
  572.6 4.9 custom-call.9
  (269 shorter events, 298.6 us)
Async XLA Ops:
  4.6 53.5 %copy-start = (bf16[2,16,64,1024]{3,2,1,0:T(8,128)(2,1)}, bf16[2,16,64,1024]{3,2,1,0:T(8,128)(2,1)S(1)}, u32[]{:S(2)}) copy-start(bf16[2,16,64,1024]{3,2,1,0:T(8,128)(2,1)S(1)} %fusion.2) | copy-start | bytes 12582916
  5.3 48.4 %collective-permute-start = (bf16[1,16,64,1024]{3,2,1,0:T(8,128)(2,1)S(1)}, bf16[1,16,64,1024]{3,2,1,0:T(8,128)(2,1)S(1)}, u32[]{:S(2)}, u32[]{:S(2)}) collective-permute-start(bf16[1,16,64,1024]{3,2,1,0:T(8,128)(2,1)S(1)} %get-tuple-element.11), channel_id=1, source_target_pairs={{0,16},{16,32},{32,48},{48,64},{64,80},{80,96},{96,112},{1,17},{17... | collective-permute-start | bytes 6291464 | tf_op jit(solution)/shard_map/ppermute | solution.py:27
  9.0 53.0 %copy-start.52 = (f32[2,16,4096]{2,1,0:T(8,128)S(1)}, f32[2,16,4096]{2,1,0:T(8,128)}, u32[]{:S(2)}) copy-start(f32[2,16,4096]{2,1,0:T(8,128)} %param.8) | copy-start | bytes 1572868
  9.0 49.1 %collective-permute-start.1 = (bf16[1,16,64,1024]{3,2,1,0:T(8,128)(2,1)S(1)}, bf16[1,16,64,1024]{3,2,1,0:T(8,128)(2,1)S(1)}, u32[]{:S(2)}, u32[]{:S(2)}) collective-permute-start(bf16[1,16,64,1024]{3,2,1,0:T(8,128)(2,1)S(1)} %get-tuple-element.12), channel_id=1, source_target_pairs={{16,0},{32,16},{48,32},{64,48},{80,64},{96,80},{112,96},{17,1},{33... | collective-permute-start | bytes 6291464 | tf_op jit(solution)/shard_map/ppermute | solution.py:28
  59.2 4.2 collective-permute-start.2
  60.5 8.2 %collective-permute-start.3 = (bf16[4,1,64,1024]{3,2,1,0:T(8,128)(2,1)}, bf16[4,1,64,1024]{3,2,1,0:T(8,128)(2,1)}, u32[]{:S(2)}, u32[]{:S(2)}) collective-permute-start(bf16[4,1,64,1024]{3,2,1,0:T(8,128)(2,1)} %get-tuple-element.10), channel_id=1, source_target_pairs={{1,0},{2,1},{3,2},{4,3},{5,4},{6,5},{7,6},{8,7},{9,8},{10,9},{11,1... | collective-permute-start | bytes 1572872 | tf_op jit(solution)/shard_map/ppermute | solution.py:28
  107.5 15.7 %copy-start.53 = (f32[2,16,4096]{2,1,0:T(8,128)S(1)}, f32[2,16,4096]{2,1,0:T(8,128)}, u32[]{:S(2)}) copy-start(f32[2,16,4096]{2,1,0:T(8,128)} %param.8) | copy-start | bytes 1572868
  112.6 15.0 %collective-permute-start.5 = (f32[1,16,4096]{2,1,0:T(8,128)}, f32[1,16,4096]{2,1,0:T(8,128)S(1)}, u32[]{:S(2)}, u32[]{:S(2)}) collective-permute-start(f32[1,16,4096]{2,1,0:T(8,128)} %slice.253), channel_id=1, source_target_pairs={{16,0},{32,16},{48,32},{64,48},{80,64},{96,80},{112,96},{17,1},{33... | collective-permute-start | bytes 786440 | tf_op jit(solution)/shard_map/ppermute | solution.py:28
  113.9 13.7 %collective-permute-start.4 = (f32[1,16,4096]{2,1,0:T(8,128)}, f32[1,16,4096]{2,1,0:T(8,128)}, u32[]{:S(2)}, u32[]{:S(2)}) collective-permute-start(f32[1,16,4096]{2,1,0:T(8,128)} %slice.251), channel_id=1, source_target_pairs={{0,16},{16,32},{32,48},{48,64},{64,80},{80,96},{96,112},{1,17},{17... | collective-permute-start | bytes 786440 | tf_op jit(solution)/shard_map/ppermute | solution.py:27
  123.3 17.3 %copy-start.28 = (f32[2,16,4096]{2,1,0:T(8,128)}, f32[2,16,4096]{2,1,0:T(8,128)S(1)}, u32[]{:S(2)}) copy-start(f32[2,16,4096]{2,1,0:T(8,128)S(1)} %mul.285) | copy-start | bytes 1572868
  123.3 21.7 %copy-start.12 = (f32[2,16,64,64]{2,3,1,0:T(8,128)S(1)}, f32[2,16,64,64]{2,3,1,0:T(8,128)}, u32[]{:S(2)}) copy-start(f32[2,16,64,64]{2,3,1,0:T(8,128)} %get-tuple-element.69) | copy-start | bytes 1572868
  129.3 21.1 %collective-permute-start.6 = (f32[4,1,4096]{2,1,0:T(1,128)}, f32[4,1,4096]{2,1,0:T(1,128)S(1)}, u32[]{:S(2)}, u32[]{:S(2)}) collective-permute-start(f32[4,1,4096]{2,1,0:T(1,128)} %get-tuple-element.45), channel_id=1, source_target_pairs={{0,1},{1,2},{2,3},{3,4},{4,5},{5,6},{6,7},{7,8},{8,9},{9,10},{10,1... | collective-permute-start | bytes 196616 | tf_op jit(solution)/shard_map/ppermute | solution.py:27
  139.3 11.1 %collective-permute-start.7 = (f32[4,1,4096]{2,1,0:T(1,128)}, f32[4,1,4096]{2,1,0:T(1,128)S(1)}, u32[]{:S(2)}, u32[]{:S(2)}) collective-permute-start(f32[4,1,4096]{2,1,0:T(1,128)} %get-tuple-element.46), channel_id=1, source_target_pairs={{1,0},{2,1},{3,2},{4,3},{5,4},{6,5},{7,6},{8,7},{9,8},{10,9},{11,1... | collective-permute-start | bytes 196616 | tf_op jit(solution)/shard_map/ppermute | solution.py:28
  271.9 16.9 %copy-start.27 = (f32[2,16,4096]{2,1,0:T(8,128)S(1)}, f32[2,16,4096]{2,1,0:T(8,128)}, u32[]{:S(2)}) copy-start(f32[2,16,4096]{2,1,0:T(8,128)} %mul.288) | copy-start | bytes 1572868
  271.9 10.8 %collective-permute-start.9 = (f32[1,16,4096]{2,1,0:T(8,128)}, f32[1,16,4096]{2,1,0:T(8,128)S(1)}, u32[]{:S(2)}, u32[]{:S(2)}) collective-permute-start(f32[1,16,4096]{2,1,0:T(8,128)} %slice.267), channel_id=1, source_target_pairs={{16,0},{32,16},{48,32},{64,48},{80,64},{96,80},{112,96},{17,1},{33... | collective-permute-start | bytes 786440 | tf_op jit(solution)/shard_map/ppermute | solution.py:28
  273.3 10.6 %collective-permute-start.8 = (f32[1,16,4096]{2,1,0:T(8,128)}, f32[1,16,4096]{2,1,0:T(8,128)S(1)}, u32[]{:S(2)}, u32[]{:S(2)}) collective-permute-start(f32[1,16,4096]{2,1,0:T(8,128)} %slice.265), channel_id=1, source_target_pairs={{0,16},{16,32},{32,48},{48,64},{64,80},{80,96},{96,112},{1,17},{17... | collective-permute-start | bytes 786440 | tf_op jit(solution)/shard_map/ppermute | solution.py:27
  285.9 13.3 %collective-permute-start.10 = (f32[4,1,4096]{2,1,0:T(1,128)}, f32[4,1,4096]{2,1,0:T(1,128)S(1)}, u32[]{:S(2)}, u32[]{:S(2)}) collective-permute-start(f32[4,1,4096]{2,1,0:T(1,128)} %get-tuple-element.39), channel_id=1, source_target_pairs={{0,1},{1,2},{2,3},{3,4},{4,5},{5,6},{6,7},{7,8},{8,9},{9,10},{10,1... | collective-permute-start | bytes 196616 | tf_op jit(solution)/shard_map/ppermute | solution.py:27
  287.1 12.0 %collective-permute-start.11 = (f32[4,1,4096]{2,1,0:T(1,128)}, f32[4,1,4096]{2,1,0:T(1,128)S(1)}, u32[]{:S(2)}, u32[]{:S(2)}) collective-permute-start(f32[4,1,4096]{2,1,0:T(1,128)} %get-tuple-element.40), channel_id=1, source_target_pairs={{1,0},{2,1},{3,2},{4,3},{5,4},{6,5},{7,6},{8,7},{9,8},{10,9},{11,1... | collective-permute-start | bytes 196616 | tf_op jit(solution)/shard_map/ppermute | solution.py:28
  419.2 15.5 %copy-start.11 = (f32[2,16,64,64]{2,3,1,0:T(8,128)S(1)}, f32[2,16,64,64]{2,3,1,0:T(8,128)}, u32[]{:S(2)}) copy-start(f32[2,16,64,64]{2,3,1,0:T(8,128)} %get-tuple-element.75) | copy-start | bytes 1572868
  428.7 16.9 %copy-start.26 = (f32[2,16,4096]{2,1,0:T(8,128)S(1)}, f32[2,16,4096]{2,1,0:T(8,128)}, u32[]{:S(2)}) copy-start(f32[2,16,4096]{2,1,0:T(8,128)} %mul.291) | copy-start | bytes 1572868
  428.7 10.8 %collective-permute-start.13 = (f32[1,16,4096]{2,1,0:T(8,128)}, f32[1,16,4096]{2,1,0:T(8,128)S(1)}, u32[]{:S(2)}, u32[]{:S(2)}) collective-permute-start(f32[1,16,4096]{2,1,0:T(8,128)} %slice.281), channel_id=1, source_target_pairs={{16,0},{32,16},{48,32},{64,48},{80,64},{96,80},{112,96},{17,1},{33... | collective-permute-start | bytes 786440 | tf_op jit(solution)/shard_map/ppermute | solution.py:28
  430.1 10.6 %collective-permute-start.12 = (f32[1,16,4096]{2,1,0:T(8,128)}, f32[1,16,4096]{2,1,0:T(8,128)S(1)}, u32[]{:S(2)}, u32[]{:S(2)}) collective-permute-start(f32[1,16,4096]{2,1,0:T(8,128)} %slice.279), channel_id=1, source_target_pairs={{0,16},{16,32},{32,48},{48,64},{64,80},{80,96},{96,112},{1,17},{17... | collective-permute-start | bytes 786440 | tf_op jit(solution)/shard_map/ppermute | solution.py:27
  442.7 13.1 %collective-permute-start.14 = (f32[4,1,4096]{2,1,0:T(1,128)}, f32[4,1,4096]{2,1,0:T(1,128)S(1)}, u32[]{:S(2)}, u32[]{:S(2)}) collective-permute-start(f32[4,1,4096]{2,1,0:T(1,128)} %get-tuple-element.33), channel_id=1, source_target_pairs={{0,1},{1,2},{2,3},{3,4},{4,5},{5,6},{6,7},{7,8},{8,9},{9,10},{10,1... | collective-permute-start | bytes 196616 | tf_op jit(solution)/shard_map/ppermute | solution.py:27
  444.0 11.8 %collective-permute-start.15 = (f32[4,1,4096]{2,1,0:T(1,128)}, f32[4,1,4096]{2,1,0:T(1,128)S(1)}, u32[]{:S(2)}, u32[]{:S(2)}) collective-permute-start(f32[4,1,4096]{2,1,0:T(1,128)} %get-tuple-element.34), channel_id=1, source_target_pairs={{1,0},{2,1},{3,2},{4,3},{5,4},{6,5},{7,6},{8,7},{9,8},{10,9},{11,1... | collective-permute-start | bytes 196616 | tf_op jit(solution)/shard_map/ppermute | solution.py:28
  (47 other events, 294.7 us)
where the time goes:
time: 588 us; the launch traced here: 581 us
  blocking collectives  182 us (31%)
  matrix products  132 us (22%)
  local copies, waits for them, and re-layouts  88.8 us (15%)
  other arithmetic  75.6 us (13%)
  waiting for transfers between devices  56.7 us (10%)
  starting transfers between devices  44 us (7%)
    psum x15, blocking collectives, by_axis(): return functools.reduce(lax.psum, axes, shard)  182 us
    dot_general x24, matrix products, local(): jnp.einsum('abpq,abqk->abpk', block, source, precision=lax.Precision.HIGH...  82.5 us
    reshape x24, local copies, waits for them, and re-layouts, local(): source = source.reshape(tile_rows, tile_cols, patches, RANK)  54.2 us
    ppermute x8, waiting for transfers between devices, with_halo(): before = lax.ppermute(last, axis, up)  45.9 us
    ppermute x8, starting transfers between devices, with_halo(): before = lax.ppermute(last, axis, up)  32.3 us
    dot_general x9, matrix products, pair_weights(): jnp.einsum('abpd,abqd->abpq', left_unit, right_unit, preferred_element_ty...  26.4 us
    another operation x9, other arithmetic, local(): lower = jnp.linalg.cholesky(gram_matrix)  19.6 us
    concatenate x7, other arithmetic, with_halo(): shard = jnp.concatenate([before, shard, after], axis=dim)  18.2 us
  transfers between devices with their start and end apart: 16, of which 7 were waited for; matrix products, arithmetic and copies ran while one was open for 8% of the time, Pallas kernels for 0%

commit v1 on v0

v1 whole, which is shorter than its diff:
```python
import functools
import math

import jax
import jax.numpy as jnp
from jax import lax
from jax.experimental import pallas as pl
from jax.experimental.pallas import tpu as pltpu
from jax.sharding import Mesh
from jax.sharding import PartitionSpec as P

RANK = 64
ITERS = 3
PATCH = 64
AXES = ("row_0", "row_1", "col_0", "col_1", "col_2")
ROW = ("row_0", "row_1")
COL = ("col_0", "col_1", "col_2")
NROW, NCOL = 8, 16
TC = 16
MESH_ID = pl.DeviceIdType.MESH
AFFINITY_TEMP = 4.0
STEPS = 8
WIDTH = TC // STEPS

DIRS = ((-1, 0), (1, 0), (0, -1), (0, 1), (-1, -1), (-1, 1), (1, -1), (1, 1))


def position():
    return tuple(lax.axis_index(a) for a in AXES)


def row_col(pos):
    return pos[0] * 4 + pos[1], pos[2] * 4 + pos[3] * 2 + pos[4]


def device_at(row, col):
    row = jnp.clip(row, 0, NROW - 1)
    col = jnp.clip(col, 0, NCOL - 1)
    return (row // 4, row % 4, col // 4, (col // 2) % 2, col % 2)


def inside(row, col):
    return (row >= 0) & (row < NROW) & (col >= 0) & (col < NCOL)


def barrier(row, col, others):
    sem = pltpu.get_barrier_semaphore()
    for dr, dc in DIRS:

        @pl.when(inside(row + dr, col + dc))
        def _(dr=dr, dc=dc):
            pl.semaphore_signal(
                sem, inc=1, device_id=device_at(row + dr, col + dc), device_id_type=MESH_ID
            )

    for other in others:
        pl.semaphore_signal(sem, inc=1, device_id=other, device_id_type=MESH_ID)
    near = sum(inside(row + dr, col + dc).astype(jnp.int32) for dr, dc in DIRS)
    pl.semaphore_wait(sem, near + len(others))


def send_slices(dr, dc, first=1, count=TC):
    if dc == 0:
        src, dst = pl.ds(first, count), pl.ds(first, count)
    elif dc < 0:
        src, dst = pl.ds(1, 1), pl.ds(TC + 1, 1)
    else:
        src, dst = pl.ds(TC, 1), pl.ds(0, 1)
    return src, dst


def halo_copy(own, halo, dr, dc, send, recv, device, first=1, count=TC):
    src, dst = send_slices(dr, dc, first, count)
    if dr == 0:
        a, b = own.at[src], own.at[dst]
    elif dr < 0:
        a, b = own.at[src, 0:PATCH], halo.at[dst, PATCH : 2 * PATCH]
    else:
        a, b = own.at[src, PATCH : 2 * PATCH], halo.at[dst, 0:PATCH]
    return pltpu.make_async_remote_copy(
        src_ref=a, dst_ref=b, send_sem=send, recv_sem=recv, device_id=device, device_id_type=MESH_ID
    )


def mask_copy(mask, dr, dc, send, recv, device):
    src, dst = send_slices(dr, dc)
    if dr == 0:
        a, b = mask.at[0:2, src], mask.at[0:2, dst]
    elif dr < 0:
        a, b = mask.at[0:1, src], mask.at[3:4, dst]
    else:
        a, b = mask.at[1:2, src], mask.at[2:3, dst]
    return pltpu.make_async_remote_copy(
        src_ref=a, dst_ref=b, send_sem=send, recv_sem=recv, device_id=device, device_id_type=MESH_ID
    )


NT = (((1,), (1,)), ((), ()))
TN = (((0,), (0,)), ((), ()))


def eye(n):
    return lax.broadcasted_iota(jnp.int32, (n, n), 0) == lax.broadcasted_iota(jnp.int32, (n, n), 1)


def affinity_kernel(
    feat, tissue, e_ref, aux_ref, own, halo, mask, deg, usend, urecv, csend, crecv, msend, mrecv
):
    row, col = row_col(position())

    for k in (2, 3):
        mask[k] = jnp.zeros((TC + 2, 8, 128), jnp.float32)
    for k in (0, 1):
        mask[k, 0] = jnp.zeros((8, 128), jnp.float32)
        mask[k, TC + 1] = jnp.zeros((8, 128), jnp.float32)
        t = tissue[k].astype(jnp.float32)
        t = jnp.concatenate([t, t], axis=1)
        for c in range(TC):
            mask[k, c + 1] = jnp.broadcast_to(t[c : c + 1, :], (8, 128))

    barrier(row, col, ())

    def edges(step, fn):
        first = 1 + step * WIDTH
        for k in (0, 1):
            dr = DIRS[k][0]
            fn(
                k,
                halo_copy(
                    own, halo, dr, 0, usend.at[k, step], urecv.at[k, step],
                    device_at(row + dr, col), first, WIDTH,
                ),
            )

    def start_edges(step):
        def go(k, copy):
            @pl.when(inside(row + DIRS[k][0], col))
            def _():
                copy.start()

        edges(step, go)

    def normalise(c):
        for k in (0, 1):
            v = feat[k, c].astype(jnp.float32)
            total = jnp.sum(v * v, axis=-1, keepdims=True)
            own[c + 1, k * PATCH : (k + 1) * PATCH] = (v * lax.rsqrt(total + 1e-06)).astype(
                jnp.bfloat16
            )

    for c in range(WIDTH):
        normalise(c)

    def group(step, _):
        for i in range(WIDTH):
            normalise(step * WIDTH + i)
        start_edges(step - 1)
        return 0

    lax.fori_loop(1, STEPS, group, 0)
    start_edges(STEPS - 1)

    def side(k):
        dr, dc = DIRS[k]
        device = device_at(row + dr, col + dc)
        return halo_copy(own, halo, dr, dc, csend.at[k], crecv.at[k], device)

    def side_mask(k):
        dr, dc = DIRS[k]
        device = device_at(row + dr, col + dc)
        return mask_copy(mask, dr, dc, msend.at[k], mrecv.at[k], device)

    for k, (dr, dc) in enumerate(DIRS):

        @pl.when(inside(row + dr, col + dc))
        def _(k=k):
            side_mask(k).start()
            if k >= 2:
                side(k).start()

    lane = lax.broadcasted_iota(jnp.int32, (128, 128), 1)
    sub = lax.broadcasted_iota(jnp.int32, (128, 128), 0)
    diagonal = lane == sub
    seen = (lane < PATCH) == (sub < PATCH)

    def block(c, cc, other, upper, lower, kind):
        s = lax.dot_general(own[c], other[cc], NT, preferred_element_type=jnp.float32)
        w = jnp.exp(AFFINITY_TEMP * (s - 1.0))
        m = jnp.where(lane[0:1] < PATCH, upper[cc, 0:1], lower[cc, 0:1])
        keep = jnp.broadcast_to(m, (128, 128)) > 0.5
        if kind == 1:
            keep = keep & seen
        return jnp.where(keep, w, 0.0)

    def own_blocks(c, parts):
        total = jnp.zeros((128, 1), jnp.float32)
        for d in parts:
            w = block(c, c + d - 1, own, mask.at[0], mask.at[1], 0)
            total = total + jnp.sum(w, axis=1, keepdims=True)
            if d == 1:
                self_w = jnp.sum(jnp.where(diagonal, w, 0.0), axis=1, keepdims=True)
                aux_ref[c - 1, :, 64:128] = jnp.broadcast_to(self_w, (128, 64))
                w = jnp.where(diagonal, 0.0, w)
            e_ref[c - 1, 0, :, d * 128 : (d + 1) * 128] = w.astype(jnp.bfloat16)
        return total

    def halo_blocks(c):
        total = jnp.zeros((128, 1), jnp.float32)
        for d in range(3):
            w = block(c, c + d - 1, halo, mask.at[2], mask.at[3], 1)
            total = total + jnp.sum(w, axis=1, keepdims=True)
            e_ref[c - 1, 1, :, d * 128 : (d + 1) * 128] = w.astype(jnp.bfloat16)
        return total

    def inner(c, _):
        deg[c] = jnp.broadcast_to(own_blocks(c, (0, 1, 2)), (128, 128))
        return 0

    lax.fori_loop(2, TC, inner, 0)

    for k, (dr, dc) in enumerate(DIRS):

        @pl.when(inside(row - dr, col - dc))
        def _(k=k):
            side_mask(k).wait_recv()
            if k >= 2:
                side(k).wait_recv()

    for c in (1, TC):
        deg[c] = jnp.broadcast_to(own_blocks(c, (0, 1, 2)), (128, 128))

    def finish(c):
        total = deg[c][:, 0:1] + halo_blocks(c)
        m = jnp.where(lane[0:1] < PATCH, mask[0, c, 0:1], mask[1, c, 0:1])
        mine = jnp.sum(jnp.where(diagonal, jnp.broadcast_to(m, (128, 128)), 0.0), axis=1, keepdims=True)
        scale = lax.rsqrt(1.0 + mine * total)
        self_w = aux_ref[c - 1, :, 64:65]
        aux_ref[c - 1, :, 0:64] = jnp.broadcast_to(scale, (128, 64))
        aux_ref[c - 1, :, 64:128] = jnp.broadcast_to(scale * mine, (128, 64))
        deg[c] = jnp.broadcast_to(1.0 + mine * scale * scale * self_w, (128, 128))

    def wait_edges(step):
        def go(k, copy):
            @pl.when(inside(row - DIRS[k][0], col))
            def _():
                copy.wait_recv()

        edges(step, go)

    wait_edges(0)
    for c in range(1, WIDTH):
        finish(c)

    def halo_group(step, _):
        wait_edges(step)
        for i in range(WIDTH):
            finish(step * WIDTH + i)
        return 0

    lax.fori_loop(1, STEPS, halo_group, 0)
    finish(TC)

    def drain(step, _):
        def go(k, copy):
            @pl.when(inside(row + DIRS[k][0], col))
            def _():
                copy.wait_send()

        edges(step, go)
        return 0

    lax.fori_loop(0, STEPS, drain, 0)
    for k, (dr, dc) in enumerate(DIRS):

        @pl.when(inside(row + dr, col + dc))
        def _(k=k):
            side_mask(k).wait_send()
            if k >= 2:
                side(k).wait_send()

    return deg


def affinity_body(
    feat, tissue, e_ref, aux_ref, diag_ref, own, halo, mask, deg, *sems
):
    affinity_kernel(feat, tissue, e_ref, aux_ref, own, halo, mask, deg, *sems)

    def put(c, _):
        diag_ref[c] = deg[c + 1][:, 0:64]
        return 0

    lax.fori_loop(0, TC, put, 0)


def stage_peers(pos):
    z = pos[3] * 2 + pos[0]
    core = (pos[4], [(pos[0], pos[1], pos[2], pos[3], 1 - pos[4])])
    x = (pos[1], [(pos[0], (pos[1] + d) % 4, pos[2], pos[3], pos[4]) for d in (1, 2, 3)])
    y = (pos[2], [(pos[0], pos[1], (pos[2] + d) % 4, pos[3], pos[4]) for d in (1, 2, 3)])
    along = [(z + d) % 4 for d in (1, 2, 3)]
    zz = (z, [(q % 2, pos[1], pos[2], q // 2, pos[4]) for q in along])
    return [core, x, y, zz]


def hi_lo(v):
    hi = v.astype(jnp.bfloat16)
    lo = (v - hi.astype(jnp.float32)).astype(jnp.bfloat16)
    return jnp.concatenate([hi, lo], axis=1)


def inverse_factor(gram):
    n = RANK
    m = jnp.concatenate([gram, jnp.where(eye(n), 1.0, 0.0)], axis=1)
    sub = lax.broadcasted_iota(jnp.int32, (n, 2 * n), 0)
    lane = lax.broadcasted_iota(jnp.int32, (n, 2 * n), 1)
    for k in range(n - 1):
        column = jnp.broadcast_to(m[:, k : k + 1], (n, 2 * n))
        pivot = column[k : k + 1, :]
        line = m[k : k + 1, :] / pivot
        m = m - jnp.where(sub > k, column, 0.0) * line
    d = jnp.sum(jnp.where(lane == sub, m, 0.0), axis=1, keepdims=True)
    return m[:, n:] * lax.rsqrt(d)


def iterate_kernel(
    e_ref, aux_ref, diag_ref, probe_ref, out_ref,
    own, halo, acc, q, pair, total, gsum, psend, precv, gsend, grecv,
):
    pos = position()
    row, col = row_col(pos)
    stages = stage_peers(pos)

    zero = jnp.zeros((128, 128), jnp.bfloat16)

    def clear(i, _):
        own[i, 0] = zero
        own[i, TC + 1] = zero

        def one(c, _):
            halo[i, c] = zero
            return 0

        lax.fori_loop(0, TC + 2, one, 0)
        return 0

    lax.fori_loop(0, ITERS, clear, 0)

    def load(c, _):
        v = probe_ref[c]
        q[c] = v
        own[0, c + 1] = hi_lo(v * aux_ref[c, :, 0:64])
        return 0

    lax.fori_loop(0, TC, load, 0)
    barrier(row, col, [p for _, peers in stages for p in peers])

    def step(t, _):
        def panel(k):
            dr, dc = DIRS[k]
            return halo_copy(
                own.at[t], halo.at[t], dr, dc, psend.at[t, k], precv.at[t, k],
                device_at(row + dr, col + dc),
            )

        for k, (dr, dc) in enumerate(DIRS):

            @pl.when(inside(row + dr, col + dc))
            def _(k=k):
                panel(k).start()

        def own_part(c, _):
            b = own[t, pl.ds(c, 3)].reshape(384, 128)
            acc[c] = jnp.dot(e_ref[c, 0], b, preferred_element_type=jnp.float32)
            return 0

        lax.fori_loop(1, TC - 1, own_part, 0)
        for k, (dr, dc) in enumerate(DIRS):

            @pl.when(inside(row - dr, col - dc))
            def _(k=k):
                panel(k).wait_recv()

        own_part(0, 0)
        own_part(TC - 1, 0)
        total[...] = jnp.zeros((128, 128), jnp.float32)

        def halo_part(c, _):
            b = halo[t, pl.ds(c, 3)].reshape(384, 128)
            v = acc[c] + jnp.dot(e_ref[c, 1], b, preferred_element_type=jnp.float32)
            v = v[:, :64] + v[:, 64:]
            y = q[c] * diag_ref[c] + aux_ref[c, :, 64:128] * v
            p = hi_lo(y)
            pair[c] = p
            total[...] += lax.dot_general(p, p, TN, preferred_element_type=jnp.float32)
            return 0

        lax.fori_loop(0, TC, halo_part, 0)
        g = total[...]
        g = g[:, :64] + g[:, 64:]
        g = g[:64] + g[64:]
        packed = jnp.concatenate([g[:32], g[32:]], axis=1)

        for s, (place, peers) in enumerate(stages):
            n = len(peers) + 1
            gsum[t, s, place] = packed

            def exchange(d, there, s=s, place=place, n=n):
                return pltpu.make_async_remote_copy(
                    src_ref=gsum.at[t, s, place],
                    dst_ref=gsum.at[t, s, place],
                    send_sem=gsend.at[t, s, d],
                    recv_sem=grecv.at[t, s, d],
                    device_id=there,
                    device_id_type=MESH_ID,
                )

            def arrival(d, there, s=s, place=place, n=n):
                origin = (place + n - 1 - d) % n
                return pltpu.make_async_remote_copy(
                    src_ref=gsum.at[t, s, place],
                    dst_ref=gsum.at[t, s, origin],
                    send_sem=gsend.at[t, s, d],
                    recv_sem=grecv.at[t, s, d],
                    device_id=there,
                    device_id_type=MESH_ID,
                )

            for d, there in enumerate(peers):
                exchange(d, there).start()
            for d, there in enumerate(peers):
                arrival(d, there).wait_recv()
            packed = gsum[t, s, 0]
            for i in range(1, n):
                packed = packed + gsum[t, s, i]

        gram = jnp.concatenate([packed[:, :64], packed[:, 64:]], axis=0)
        inv = inverse_factor(gram)
        hi = inv.astype(jnp.bfloat16)
        lo = (inv - hi.astype(jnp.float32)).astype(jnp.bfloat16)
        both = jnp.concatenate(
            [jnp.concatenate([hi, hi], axis=1), jnp.concatenate([lo, lo], axis=1)], axis=0
        )

        def solve(c):
            v = lax.dot_general(pair[c], both, NT, preferred_element_type=jnp.float32)
            return v[:, :64] + v[:, 64:]

        @pl.when(t < ITERS - 1)
        def _():
            def renew(c, _):
                v = solve(c)
                q[c] = v
                own[t + 1, c + 1] = hi_lo(v * aux_ref[c, :, 0:64])
                return 0

            lax.fori_loop(0, TC, renew, 0)

        @pl.when(t == ITERS - 1)
        def _():
            factor = math.sqrt(float(NROW * 2 * NCOL * TC * PATCH))

            def last(c, _):
                out_ref[c] = factor * solve(c)
                return 0

            lax.fori_loop(0, TC, last, 0)

        for k, (dr, dc) in enumerate(DIRS):

            @pl.when(inside(row + dr, col + dc))
            def _(k=k):
                panel(k).wait_send()

        for s, (place, peers) in enumerate(stages):
            for d, there in enumerate(peers):
                pltpu.make_async_remote_copy(
                    src_ref=gsum.at[t, s, place],
                    dst_ref=gsum.at[t, s, place],
                    send_sem=gsend.at[t, s, d],
                    recv_sem=grecv.at[t, s, d],
                    device_id=there,
                    device_id_type=MESH_ID,
                ).wait_send()
        return 0

    lax.fori_loop(0, ITERS, step, 0)


VM = pl.BlockSpec(memory_space=pltpu.VMEM)
DMA = pltpu.SemaphoreType.DMA
LIMIT = 60 * 2**20


def local(features, tissue, probe):
    width = features.shape[-1]
    e, aux, diag = pl.pallas_call(
        affinity_body,
        out_shape=(
            jax.ShapeDtypeStruct((TC, 2, 128, 384), jnp.bfloat16),
            jax.ShapeDtypeStruct((TC, 128, 128), jnp.float32),
            jax.ShapeDtypeStruct((TC, 128, 64), jnp.float32),
        ),
        in_specs=[VM, VM],
        out_specs=(VM, VM, VM),
        scratch_shapes=[
            pltpu.VMEM((TC + 2, 128, width), jnp.bfloat16),
            pltpu.VMEM((TC + 2, 128, width), jnp.bfloat16),
            pltpu.VMEM((4, TC + 2, 8, 128), jnp.float32),
            pltpu.VMEM((TC + 1, 128, 128), jnp.float32),
            DMA((2, STEPS)), DMA((2, STEPS)), DMA((8,)), DMA((8,)), DMA((8,)), DMA((8,)),
        ],
        compiler_params=pltpu.CompilerParams(
            collective_id=0, has_side_effects=True, vmem_limit_bytes=LIMIT
        ),
        name="affinity",
    )(features, tissue)
    panel = probe.reshape(2, TC, PATCH, RANK).transpose(1, 0, 2, 3).reshape(TC, 128, RANK)
    out = pl.pallas_call(
        iterate_kernel,
        out_shape=jax.ShapeDtypeStruct((TC, 128, RANK), jnp.float32),
        in_specs=[VM] * 4,
        out_specs=VM,
        scratch_shapes=[
            pltpu.VMEM((ITERS, TC + 2, 128, 128), jnp.bfloat16),
            pltpu.VMEM((ITERS, TC + 2, 128, 128), jnp.bfloat16),
            pltpu.VMEM((TC, 128, 128), jnp.float32),
            pltpu.VMEM((TC, 128, RANK), jnp.float32),
            pltpu.VMEM((TC, 128, 128), jnp.bfloat16),
            pltpu.VMEM((128, 128), jnp.float32),
            pltpu.VMEM((ITERS, 4, 4, 32, 128), jnp.float32),
            DMA((ITERS, 8)), DMA((ITERS, 8)), DMA((ITERS, 4, 3)), DMA((ITERS, 4, 3)),
        ],
        compiler_params=pltpu.CompilerParams(
            collective_id=1, has_side_effects=True, vmem_limit_bytes=LIMIT
        ),
        name="iterate",
    )(e, aux, diag, panel)
    return out.reshape(TC, 2, PATCH, RANK).transpose(1, 0, 2, 3).reshape(2, TC, PATCH * RANK)


def solution(mesh):
    torus = Mesh(mesh.devices.reshape(2, 4, 4, 2, 2), AXES)
    return jax.shard_map(
        local,
        mesh=torus,
        in_specs=(P(ROW, COL, None, None), P(ROW, COL, None), P(ROW, COL, None)),
        out_specs=P(ROW, COL, None),
        check_vma=False,
    )
```

time: 588 us -> 217 us (0.37); the launches traced: 581 us -> 217 us
  Pallas kernels: 0 us -> 211 us
  blocking collectives: 182 us -> 0 us
  matrix products: 132 us -> 0 us
  local copies, waits for them, and re-layouts: 88.8 us -> 5.39 us
  other arithmetic: 75.6 us -> 0 us
  waiting for transfers between devices: 56.7 us -> 0 us
  starting transfers between devices: 44 us -> 0 us
    pallas_call x0 -> x2, Pallas kernels: none -> 211 us  [the longest x1 143 us: local(): pl.pallas_call(iterate_kernel, out_shape=jax.ShapeDtypeStruct((TC, 128, R...]
    psum x15 -> x0, blocking collectives: 182 us -> none  [by_axis(): return functools.reduce(lax.psum, axes, shard)]
    dot_general x39 -> x0, matrix products: 127 us -> none  [the longest x24 82.5 us: local(): jnp.einsum('abpq,abqk->abpk', block, source, precision=lax.Precision.HIGH...]
    ppermute x16 -> x0, waiting for transfers between devices: 56.7 us -> none  [the longest x8 45.9 us: with_halo(): before = lax.ppermute(last, axis, up)]
    reshape x27 -> x4, local copies, waits for them, and re-layouts: 58 us -> 5.39 us  [the longest x2 2.85 us: local(): out.reshape(TC, 2, PATCH, RANK).transpose(1, 0, 2, 3)]
    ppermute x16 -> x0, starting transfers between devices: 44 us -> none  [the longest x8 32.3 us: with_halo(): before = lax.ppermute(last, axis, up)]
    another operation x15 -> x0, other arithmetic: 36.2 us -> none  [the longest x9 19.6 us: local(): lower = jnp.linalg.cholesky(gram_matrix)]
    slice x16 -> x0, local copies, waits for them, and re-layouts: 20.3 us -> none  [the longest x7 9.5 us: with_halo(): last = lax.slice_in_dim(shard, length - width, length, axis=dim)]
  transfers between devices with their start and end apart: 16 -> 0, of which waited for: 7 -> 0; matrix products, arithmetic and copies ran while one was open for 8% -> 0% of each run, Pallas kernels for 0% -> 0%
where the time goes in v1:
time: 217 us
  Pallas kernels  211 us (97%)
  local copies, waits for them, and re-layouts  5.39 us (2%)
    pallas_call x1, Pallas kernels, local(): pl.pallas_call(iterate_kernel, out_shape=jax.ShapeDtypeStruct((TC, 128, R...  143 us
    pallas_call x1, Pallas kernels, local(): pl.pallas_call(affinity_body, out_shape=(jax.ShapeDtypeStruct((TC, 2, 128...  67.8 us

profile of v1, /device:TPU:0, one launch (start us, length us, event | category | flops | bytes accessed | tf_op | source)
XLA Modules:
  0.0 216.6 jit_solution(17621808557567499235)
XLA Ops:
  0.0 1.5 reshape.12
  1.5 1.1 copy.4
  2.5 67.8 %affinity.1 = (bf16[16,2,128,384]{3,2,1,0:T(8,128)(2,1)}, f32[16,128,128]{2,1,0:T(8,128)}, f32[16,128,64]{2,1,0:T(8,128)}) custom-call(bf16[2,16,64,1024]{3,2,1,0:T(8,128)(2,1)} %feat.1, s32[2,16,64]{2,1,0:T(8,128)} %tissue.1), custom_call_target="tpu_custom_call" | custom-call | tf_op jit(solution)/shard_map/affinity/pallas_call | solution.py:497
  70.3 143.4 %iterate.1 = f32[16,128,64]{2,1,0:T(8,128)} custom-call(bf16[16,2,128,384]{3,2,1,0:T(8,128)(2,1)} %get-tuple-element.8.e_ref, f32[16,128,128]{2,1,0:T(8,128)} %get-tuple-element.9.aux_ref, f32[16,128,64]{2,1,0:T(8,128)} %get-tuple-element.10.diag_ref, f32[16,128,64]{2,1,0:T(8,128)} %bitcast.10), custom_call_target="tpu_custom_call" | custom-call | tf_op jit(solution)/shard_map/iterate/pallas_call | solution.py:519
  213.7 1.7 reshape.16
  215.5 1.1 copy.6

commit v2 on v1

--- a/solution.py
+++ b/solution.py
@@ -103,10 +103,10 @@
     return lax.broadcasted_iota(jnp.int32, (n, n), 0) == lax.broadcasted_iota(jnp.int32, (n, n), 1)
 
 
-def affinity_kernel(
-    feat, tissue, e_ref, aux_ref, own, halo, mask, deg, usend, urecv, csend, crecv, msend, mrecv
+def affinity(
+    row, col, feat, tissue, e_ref, scale_ref, mine_ref, diag_ref, own, halo, mask, deg,
+    usend, urecv, csend, crecv, msend, mrecv, ready, meanwhile,
 ):
-    row, col = row_col(position())
 
     for k in (2, 3):
         mask[k] = jnp.zeros((TC + 2, 8, 128), jnp.float32)
@@ -118,7 +118,7 @@
         for c in range(TC):
             mask[k, c + 1] = jnp.broadcast_to(t[c : c + 1, :], (8, 128))
 
-    barrier(row, col, ())
+    ready()
 
     def edges(step, fn):
         first = 1 + step * WIDTH
@@ -199,7 +199,7 @@
             total = total + jnp.sum(w, axis=1, keepdims=True)
             if d == 1:
                 self_w = jnp.sum(jnp.where(diagonal, w, 0.0), axis=1, keepdims=True)
-                aux_ref[c - 1, :, 64:128] = jnp.broadcast_to(self_w, (128, 64))
+                diag_ref[c - 1] = jnp.broadcast_to(self_w, (128, 128))
                 w = jnp.where(diagonal, 0.0, w)
             e_ref[c - 1, 0, :, d * 128 : (d + 1) * 128] = w.astype(jnp.bfloat16)
         return total
@@ -216,7 +216,8 @@
         deg[c] = jnp.broadcast_to(own_blocks(c, (0, 1, 2)), (128, 128))
         return 0
 
-    lax.fori_loop(2, TC, inner, 0)
+    meanwhile()
+    lax.fori_loop(2, TC, inner, 0, unroll=2)
 
     for k, (dr, dc) in enumerate(DIRS):
 
@@ -234,10 +235,10 @@
         m = jnp.where(lane[0:1] < PATCH, mask[0, c, 0:1], mask[1, c, 0:1])
         mine = jnp.sum(jnp.where(diagonal, jnp.broadcast_to(m, (128, 128)), 0.0), axis=1, keepdims=True)
         scale = lax.rsqrt(1.0 + mine * total)
-        self_w = aux_ref[c - 1, :, 64:65]
-        aux_ref[c - 1, :, 0:64] = jnp.broadcast_to(scale, (128, 64))
-        aux_ref[c - 1, :, 64:128] = jnp.broadcast_to(scale * mine, (128, 64))
-        deg[c] = jnp.broadcast_to(1.0 + mine * scale * scale * self_w, (128, 128))
+        self_w = diag_ref[c - 1]
+        scale_ref[c - 1] = jnp.broadcast_to(scale, (128, 128))
+        mine_ref[c - 1] = jnp.broadcast_to(scale * mine, (128, 128))
+        diag_ref[c - 1] = 1.0 + (mine * scale * scale) * self_w
 
     def wait_edges(step):
         def go(k, copy):
@@ -277,20 +278,6 @@
             side_mask(k).wait_send()
             if k >= 2:
                 side(k).wait_send()
-
-    return deg
-
-
-def affinity_body(
-    feat, tissue, e_ref, aux_ref, diag_ref, own, halo, mask, deg, *sems
-):
-    affinity_kernel(feat, tissue, e_ref, aux_ref, own, halo, mask, deg, *sems)
-
-    def put(c, _):
-        diag_ref[c] = deg[c + 1][:, 0:64]
-        return 0
-
-    lax.fori_loop(0, TC, put, 0)
 
 
 def stage_peers(pos):
@@ -300,13 +287,7 @@
     y = (pos[2], [(pos[0], pos[1], (pos[2] + d) % 4, pos[3], pos[4]) for d in (1, 2, 3)])
     along = [(z + d) % 4 for d in (1, 2, 3)]
     zz = (z, [(q % 2, pos[1], pos[2], q // 2, pos[4]) for q in along])
-    return [core, x, y, zz]
-
-
-def hi_lo(v):
-    hi = v.astype(jnp.bfloat16)
-    lo = (v - hi.astype(jnp.float32)).astype(jnp.bfloat16)
-    return jnp.concatenate([hi, lo], axis=1)
+    return [core, y, zz, x]
 
 
 def inverse_factor(gram):
@@ -323,14 +304,22 @@
     return m[:, n:] * lax.rsqrt(d)
 
 
-def iterate_kernel(
-    e_ref, aux_ref, diag_ref, probe_ref, out_ref,
-    own, halo, acc, q, pair, total, gsum, psend, precv, gsend, grecv,
+def pair_of(v, low):
+    hi = v.astype(jnp.bfloat16)
+    lo = (v - hi.astype(jnp.float32)).astype(jnp.bfloat16)
+    return jnp.where(low, hi, lo)
+
+
+def kernel(
+    feat, tissue, probe, out_ref,
+    ufeat, hfeat, mask, deg, e_ref, scale_ref, mine_ref, diag_ref,
+    own, halo, acc, y, pair, total, gsum,
+    usend, urecv, csend, crecv, msend, mrecv, psend, precv, gsend, grecv,
 ):
     pos = position()
     row, col = row_col(pos)
     stages = stage_peers(pos)
-
+    low = lax.broadcasted_iota(jnp.int32, (128, 128), 1) < RANK
     zero = jnp.zeros((128, 128), jnp.bfloat16)
 
     def clear(i, _):
@@ -341,137 +330,184 @@
             halo[i, c] = zero
             return 0
 
-        lax.fori_loop(0, TC + 2, one, 0)
+        lax.fori_loop(0, TC + 2, one, 0, unroll=6)
         return 0
 
     lax.fori_loop(0, ITERS, clear, 0)
 
-    def load(c, _):
-        v = probe_ref[c]
-        q[c] = v
-        own[0, c + 1] = hi_lo(v * aux_ref[c, :, 0:64])
-        return 0
-
-    lax.fori_loop(0, TC, load, 0)
-    barrier(row, col, [p for _, peers in stages for p in peers])
-
-    def step(t, _):
-        def panel(k):
-            dr, dc = DIRS[k]
-            return halo_copy(
-                own.at[t], halo.at[t], dr, dc, psend.at[t, k], precv.at[t, k],
-                device_at(row + dr, col + dc),
-            )
-
+    def ready():
+        barrier(row, col, [p for _, peers in stages for p in peers])
+
+    def meanwhile():
+        def load(c, _):
+            for k in (0, 1):
+                v = probe[k, c]
+                y[c, k * PATCH : (k + 1) * PATCH] = jnp.concatenate([v, v], axis=1)
+            return 0
+
+        lax.fori_loop(0, TC, load, 0, unroll=4)
+
+    affinity(
+        row, col, feat, tissue, e_ref, scale_ref, mine_ref, diag_ref, ufeat, hfeat, mask, deg,
+        usend, urecv, csend, crecv, msend, mrecv, ready, meanwhile,
+    )
+
+    def panel(t, k):
+        dr, dc = DIRS[k]
+        return halo_copy(
+            own.at[t], halo.at[t], dr, dc, psend.at[t, k], precv.at[t, k],
+            device_at(row + dr, col + dc),
+        )
+
+    def each_target(fn):
         for k, (dr, dc) in enumerate(DIRS):
 
             @pl.when(inside(row + dr, col + dc))
             def _(k=k):
-                panel(k).start()
-
-        def own_part(c, _):
+                fn(k)
+
+    def each_source(fn):
+        for k, (dr, dc) in enumerate(DIRS):
+
+            @pl.when(inside(row - dr, col - dc))
+            def _(k=k):
+                fn(k)
+
+    def own_part(t, first, stop):
+        def go(c, _):
             b = own[t, pl.ds(c, 3)].reshape(384, 128)
             acc[c] = jnp.dot(e_ref[c, 0], b, preferred_element_type=jnp.float32)
             return 0
 
-        lax.fori_loop(1, TC - 1, own_part, 0)
-        for k, (dr, dc) in enumerate(DIRS):
-
-            @pl.when(inside(row - dr, col - dc))
-            def _(k=k):
-                panel(k).wait_recv()
-
-        own_part(0, 0)
-        own_part(TC - 1, 0)
-        total[...] = jnp.zeros((128, 128), jnp.float32)
-
-        def halo_part(c, _):
-            b = halo[t, pl.ds(c, 3)].reshape(384, 128)
-            v = acc[c] + jnp.dot(e_ref[c, 1], b, preferred_element_type=jnp.float32)
-            v = v[:, :64] + v[:, 64:]
-            y = q[c] * diag_ref[c] + aux_ref[c, :, 64:128] * v
-            p = hi_lo(y)
+        lax.fori_loop(first, stop, go, 0, unroll=stop - first)
+
+    def product(t, c):
+        b = halo[t, pl.ds(c, 3)].reshape(384, 128)
+        v = acc[c] + jnp.dot(e_ref[c, 1], b, preferred_element_type=jnp.float32)
+        v = v + pltpu.roll(v, RANK, 1)
+        return y[c] * diag_ref[c] + mine_ref[c] * v
+
+    def start_stage(t, s, packed):
+        place, peers = stages[s]
+        gsum[t, s, place] = packed
+        for d, there in enumerate(peers):
+            pltpu.make_async_remote_copy(
+                src_ref=gsum.at[t, s, place],
+                dst_ref=gsum.at[t, s, place],
+                send_sem=gsend.at[t, s, d],
+                recv_sem=grecv.at[t, s, d],
+                device_id=there,
+                device_id_type=MESH_ID,
+            ).start()
+
+    def end_stage(t, s):
+        place, peers = stages[s]
+        n = len(peers) + 1
+        for d, there in enumerate(peers):
+            pltpu.make_async_remote_copy(
+                src_ref=gsum.at[t, s, place],
+                dst_ref=gsum.at[t, s, (place + n - 1 - d) % n],
+                send_sem=gsend.at[t, s, d],
+                recv_sem=grecv.at[t, s, d],
+                device_id=there,
+                device_id_type=MESH_ID,
+            ).wait_recv()
+        packed = gsum[t, s, 0]
+        for i in range(1, n):
+            packed = packed + gsum[t, s, i]
+        return packed
+
+    def new_rows(t, c, v):
+        p = pair_of(v, low)
+        total[...] += lax.dot_general(p, p, TN, preferred_element_type=jnp.float32)
+        if t < ITERS - 1:
+            y[c] = v
+            own[t + 1, c + 1] = pair_of(v * scale_ref[c], low)
+        else:
             pair[c] = p
-            total[...] += lax.dot_general(p, p, TN, preferred_element_type=jnp.float32)
-            return 0
-
-        lax.fori_loop(0, TC, halo_part, 0)
+
+    def solver(packed):
+        gram = jnp.concatenate([packed[:, :64], packed[:, 64:]], axis=0)
+        inv = inverse_factor(gram)
+        hi = inv.astype(jnp.bfloat16)
+        lo = (inv - hi.astype(jnp.float32)).astype(jnp.bfloat16)
+        both = jnp.concatenate([hi, hi, lo, lo], axis=1)
+        both = jnp.concatenate([both, both], axis=0)
+
+        def solve(p):
+            p = jnp.concatenate([p, p], axis=1)
+            return lax.dot_general(p, both, NT, preferred_element_type=jnp.float32)
+
+        return solve
+
+    def first(c, _):
+        own[0, c + 1] = pair_of(y[c] * scale_ref[c], low)
+        return 0
+
+    lax.fori_loop(0, TC, first, 0, unroll=4)
+    each_target(lambda k: panel(0, k).start())
+    own_part(0, 1, TC - 1)
+    each_source(lambda k: panel(0, k).wait_recv())
+    own_part(0, 0, 1)
+    own_part(0, TC - 1, TC)
+    total[...] = jnp.zeros((128, 128), jnp.float32)
+
+    def rows0(c, _):
+        new_rows(0, c, product(0, c))
+        return 0
+
+    lax.fori_loop(0, TC, rows0, 0, unroll=8)
+
+    solve = None
+    for t in range(ITERS):
         g = total[...]
         g = g[:, :64] + g[:, 64:]
         g = g[:64] + g[64:]
         packed = jnp.concatenate([g[:32], g[32:]], axis=1)
-
-        for s, (place, peers) in enumerate(stages):
-            n = len(peers) + 1
-            gsum[t, s, place] = packed
-
-            def exchange(d, there, s=s, place=place, n=n):
-                return pltpu.make_async_remote_copy(
-                    src_ref=gsum.at[t, s, place],
-                    dst_ref=gsum.at[t, s, place],
-                    send_sem=gsend.at[t, s, d],
-                    recv_sem=grecv.at[t, s, d],
-                    device_id=there,
-                    device_id_type=MESH_ID,
-                )
-
-            def arrival(d, there, s=s, place=place, n=n):
-                origin = (place + n - 1 - d) % n
-                return pltpu.make_async_remote_copy(
-                    src_ref=gsum.at[t, s, place],
-                    dst_ref=gsum.at[t, s, origin],
-                    send_sem=gsend.at[t, s, d],
-                    recv_sem=grecv.at[t, s, d],
-                    device_id=there,
-                    device_id_type=MESH_ID,
-                )
-
-            for d, there in enumerate(peers):
-                exchange(d, there).start()
-            for d, there in enumerate(peers):
-                arrival(d, there).wait_recv()
-            packed = gsum[t, s, 0]
-            for i in range(1, n):
-                packed = packed + gsum[t, s, i]
-
-        gram = jnp.concatenate([packed[:, :64], packed[:, 64:]], axis=0)
-        inv = inverse_factor(gram)
-        hi = inv.astype(jnp.bfloat16)
-        lo = (inv - hi.astype(jnp.float32)).astype(jnp.bfloat16)
-        both = jnp.concatenate(
-            [jnp.concatenate([hi, hi], axis=1), jnp.concatenate([lo, lo], axis=1)], axis=0
-        )
-
-        def solve(c):
-            v = lax.dot_general(pair[c], both, NT, preferred_element_type=jnp.float32)
-            return v[:, :64] + v[:, 64:]
-
-        @pl.when(t < ITERS - 1)
-        def _():
-            def renew(c, _):
-                v = solve(c)
-                q[c] = v
-                own[t + 1, c + 1] = hi_lo(v * aux_ref[c, :, 0:64])
+        more = t < ITERS - 1
+        start_stage(t, 0, packed)
+        if more:
+            each_target(lambda k: panel(t + 1, k).start())
+            own_part(t + 1, 1, 5)
+        start_stage(t, 1, end_stage(t, 0))
+        if more:
+            own_part(t + 1, 5, 10)
+        start_stage(t, 2, end_stage(t, 1))
+        if more:
+            own_part(t + 1, 10, TC - 1)
+        start_stage(t, 3, end_stage(t, 2))
+        if more:
+            each_source(lambda k: panel(t + 1, k).wait_recv())
+            own_part(t + 1, 0, 1)
+            own_part(t + 1, TC - 1, TC)
+
+            def apply(c, _):
+                pair[c] = pair_of(product(t + 1, c), low)
                 return 0
 
-            lax.fori_loop(0, TC, renew, 0)
-
-        @pl.when(t == ITERS - 1)
-        def _():
-            factor = math.sqrt(float(NROW * 2 * NCOL * TC * PATCH))
-
-            def last(c, _):
-                out_ref[c] = factor * solve(c)
+            lax.fori_loop(0, TC, apply, 0, unroll=8)
+        solve = solver(end_stage(t, 3))
+        if more:
+            total[...] = jnp.zeros((128, 128), jnp.float32)
+
+            def rows(c, _):
+                new_rows(t + 1, c, solve(pair[c]))
                 return 0
 
-            lax.fori_loop(0, TC, last, 0)
-
-        for k, (dr, dc) in enumerate(DIRS):
-
-            @pl.when(inside(row + dr, col + dc))
-            def _(k=k):
-                panel(k).wait_send()
-
+            lax.fori_loop(0, TC, rows, 0, unroll=8)
+
+    factor = math.sqrt(float(NROW * 2 * NCOL * TC * PATCH))
+
+    def last(c, _):
+        v = factor * solve(pair[c])
+        for k in (0, 1):
+            out_ref[k, c] = v[k * PATCH : (k + 1) * PATCH, :RANK]
+        return 0
+
+    lax.fori_loop(0, TC, last, 0, unroll=4)
+
+    for t in range(ITERS):
+        each_target(lambda k: panel(t, k).wait_send())
         for s, (place, peers) in enumerate(stages):
             for d, there in enumerate(peers):
                 pltpu.make_async_remote_copy(
@@ -482,9 +518,6 @@
                     device_id=there,
                     device_id_type=MESH_ID,
                 ).wait_send()
-        return 0
-
-    lax.fori_loop(0, ITERS, step, 0)
 
 
 VM = pl.BlockSpec(memory_space=pltpu.VMEM)
@@ -494,49 +527,38 @@
 
 def local(features, tissue, probe):
     width = features.shape[-1]
-    e, aux, diag = pl.pallas_call(
-        affinity_body,
-        out_shape=(
-            jax.ShapeDtypeStruct((TC, 2, 128, 384), jnp.bfloat16),
-            jax.ShapeDtypeStruct((TC, 128, 128), jnp.float32),
-            jax.ShapeDtypeStruct((TC, 128, 64), jnp.float32),
-        ),
-        in_specs=[VM, VM],
-        out_specs=(VM, VM, VM),
+    full = (TC, 128, 128)
+    wide = (TC + 2, 128, width)
+    out = pl.pallas_call(
+        kernel,
+        out_shape=jax.ShapeDtypeStruct((2, TC, PATCH, RANK), jnp.float32),
+        in_specs=[VM] * 3,
+        out_specs=VM,
         scratch_shapes=[
-            pltpu.VMEM((TC + 2, 128, width), jnp.bfloat16),
-            pltpu.VMEM((TC + 2, 128, width), jnp.bfloat16),
+            pltpu.VMEM(wide, jnp.bfloat16),
+            pltpu.VMEM(wide, jnp.bfloat16),
             pltpu.VMEM((4, TC + 2, 8, 128), jnp.float32),
             pltpu.VMEM((TC + 1, 128, 128), jnp.float32),
+            pltpu.VMEM((TC, 2, 128, 384), jnp.bfloat16),
+            pltpu.VMEM(full, jnp.float32),
+            pltpu.VMEM(full, jnp.float32),
+            pltpu.VMEM(full, jnp.float32),
+            pltpu.VMEM((ITERS, TC + 2, 128, 128), jnp.bfloat16),
+            pltpu.VMEM((ITERS, TC + 2, 128, 128), jnp.bfloat16),
+            pltpu.VMEM(full, jnp.float32),
+            pltpu.VMEM(full, jnp.float32),
+            pltpu.VMEM(full, jnp.bfloat16),
+            pltpu.VMEM((128, 128), jnp.float32),
+            pltpu.VMEM((ITERS, 4, 4, 32, 128), jnp.float32),
             DMA((2, STEPS)), DMA((2, STEPS)), DMA((8,)), DMA((8,)), DMA((8,)), DMA((8,)),
+            DMA((ITERS, 8)), DMA((ITERS, 8)), DMA((ITERS, 4, 3)), DMA((ITERS, 4, 3)),
         ],
         compiler_params=pltpu.CompilerParams(
             collective_id=0, has_side_effects=True, vmem_limit_bytes=LIMIT
         ),
-        name="affinity",
-    )(features, tissue)
-    panel = probe.reshape(2, TC, PATCH, RANK).transpose(1, 0, 2, 3).reshape(TC, 128, RANK)
-    out = pl.pallas_call(
-        iterate_kernel,
-        out_shape=jax.ShapeDtypeStruct((TC, 128, RANK), jnp.float32),
-        in_specs=[VM] * 4,
-        out_specs=VM,
-        scratch_shapes=[
-            pltpu.VMEM((ITERS, TC + 2, 128, 128), jnp.bfloat16),
-            pltpu.VMEM((ITERS, TC + 2, 128, 128), jnp.bfloat16),
-            pltpu.VMEM((TC, 128, 128), jnp.float32),
-            pltpu.VMEM((TC, 128, RANK), jnp.float32),
-            pltpu.VMEM((TC, 128, 128), jnp.bfloat16),
-            pltpu.VMEM((128, 128), jnp.float32),
-            pltpu.VMEM((ITERS, 4, 4, 32, 128), jnp.float32),
-            DMA((ITERS, 8)), DMA((ITERS, 8)), DMA((ITERS, 4, 3)), DMA((ITERS, 4, 3)),
-        ],
-        compiler_params=pltpu.CompilerParams(
-            collective_id=1, has_side_effects=True, vmem_limit_bytes=LIMIT
-        ),
-        name="iterate",
-    )(e, aux, diag, panel)
-    return out.reshape(TC, 2, PATCH, RANK).transpose(1, 0, 2, 3).reshape(2, TC, PATCH * RANK)
+        name="range_finder",
+    )(features, tissue, probe.reshape(2, TC, PATCH, RANK))
+    return out.reshape(2, TC, PATCH * RANK)
 
 
 def solution(mesh):

time: 217 us -> 159 us (0.73)
  Pallas kernels: 211 us -> 154 us
    pallas_call x2 -> x1, Pallas kernels: 211 us -> 154 us  [local(): pl.pallas_call(kernel, out_shape=jax.ShapeDtypeStruct((2, TC, PATCH, RANK...]
    reshape x4 -> x2, local copies, waits for them, and re-layouts: 5.39 us -> 4.83 us  [the longest x1 2.45 us: local(): probe.reshape(2, TC, PATCH, RANK)]
where the time goes in v2:
time: 159 us
  Pallas kernels  154 us (97%)
  local copies, waits for them, and re-layouts  4.83 us (3%)
    pallas_call x1, Pallas kernels, local(): pl.pallas_call(kernel, out_shape=jax.ShapeDtypeStruct((2, TC, PATCH, RANK...  154 us

profile of v2, /device:TPU:0, one launch (start us, length us, event | category | flops | bytes accessed | tf_op | source)
XLA Modules:
  0.0 159.1 jit_solution(352105863813637716)
XLA Ops:
  0.0 2.5 %reshape.6.probe = f32[2,16,64,64]{3,2,1,0:T(8,128)} reshape(f32[2,16,4096]{2,1,0:T(8,128)} %param.5) | data formatting | bytes 1048576 | tf_op jit(solution)/shard_map/reshape | solution.py:560
  2.5 154.2 %range_finder.1 = f32[2,16,64,64]{3,2,1,0:T(8,128)} custom-call(bf16[2,16,64,1024]{3,2,1,0:T(8,128)(2,1)} %feat.1, s32[2,16,64]{2,1,0:T(8,128)} %tissue.1, f32[2,16,64,64]{3,2,1,0:T(8,128)} %reshape.6.probe), custom_call_target="tpu_custom_call" | custom-call | tf_op jit(solution)/shard_map/range_finder/pallas_call | solution.py:532
  156.7 2.4 %reshape.7 = f32[2,16,4096]{2,1,0:T(8,128)} reshape(f32[2,16,64,64]{3,2,1,0:T(8,128)} %range_finder.1) | data formatting | bytes 1048576 | tf_op jit(solution)/shard_map/reshape | solution.py:561

commit v3 on v2

--- a/solution.py
+++ b/solution.py
@@ -19,8 +19,6 @@
 TC = 16
 MESH_ID = pl.DeviceIdType.MESH
 AFFINITY_TEMP = 4.0
-STEPS = 8
-WIDTH = TC // STEPS
 
 DIRS = ((-1, 0), (1, 0), (0, -1), (0, 1), (-1, -1), (-1, 1), (1, -1), (1, 1))
 
@@ -104,10 +102,9 @@
 
 
 def affinity(
-    row, col, feat, tissue, e_ref, scale_ref, mine_ref, diag_ref, own, halo, mask, deg,
-    usend, urecv, csend, crecv, msend, mrecv, ready, meanwhile,
+    row, col, feat, tissue, e_ref, eh_ref, scale_ref, mine_ref, diag_ref, own, halo, mask, deg, served,
+    fsend, frecv, csend, crecv, msend, mrecv, rsend, rrecv, ready, meanwhile,
 ):
-
     for k in (2, 3):
         mask[k] = jnp.zeros((TC + 2, 8, 128), jnp.float32)
     for k in (0, 1):
@@ -118,121 +115,200 @@
         for c in range(TC):
             mask[k, c + 1] = jnp.broadcast_to(t[c : c + 1, :], (8, 128))
 
+    def nothing(c, _):
+        for side in (0, 1):
+            eh_ref[side, c] = jnp.zeros((PATCH, 256), jnp.bfloat16)
+        return 0
+
+    lax.fori_loop(0, TC, nothing, 0, unroll=4)
     ready()
 
-    def edges(step, fn):
-        first = 1 + step * WIDTH
-        for k in (0, 1):
-            dr = DIRS[k][0]
-            fn(
-                k,
-                halo_copy(
-                    own, halo, dr, 0, usend.at[k, step], urecv.at[k, step],
-                    device_at(row + dr, col), first, WIDTH,
-                ),
-            )
-
-    def start_edges(step):
-        def go(k, copy):
-            @pl.when(inside(row + DIRS[k][0], col))
-            def _():
-                copy.start()
-
-        edges(step, go)
+    there = [inside(row - 1, col), inside(row + 1, col)]
+    device = [device_at(row - 1, col), device_at(row + 1, col)]
+
+    def tile_copy(side, c):
+        return pltpu.make_async_remote_copy(
+            src_ref=own.at[c, side * PATCH : (side + 1) * PATCH],
+            dst_ref=halo.at[c, (1 - side) * PATCH : (2 - side) * PATCH],
+            send_sem=fsend.at[side, c],
+            recv_sem=frecv.at[1 - side, c],
+            device_id=device[side],
+            device_id_type=MESH_ID,
+        )
+
+    def tile_arrival(side, c):
+        return pltpu.make_async_remote_copy(
+            src_ref=own.at[c, side * PATCH : (side + 1) * PATCH],
+            dst_ref=halo.at[c, side * PATCH : (side + 1) * PATCH],
+            send_sem=fsend.at[side, c],
+            recv_sem=frecv.at[side, c],
+            device_id=device[side],
+            device_id_type=MESH_ID,
+        )
+
+    def weights_copy(side, c):
+        return pltpu.make_async_remote_copy(
+            src_ref=served.at[side, c - 1],
+            dst_ref=eh_ref.at[1 - side, c - 1],
+            send_sem=rsend.at[side, c],
+            recv_sem=rrecv.at[1 - side, c],
+            device_id=device[side],
+            device_id_type=MESH_ID,
+        )
+
+    def weights_arrival(side, c):
+        return pltpu.make_async_remote_copy(
+            src_ref=served.at[side, c - 1],
+            dst_ref=eh_ref.at[side, c - 1],
+            send_sem=rsend.at[side, c],
+            recv_sem=rrecv.at[side, c],
+            device_id=device[side],
+            device_id_type=MESH_ID,
+        )
+
+    def on(side, fn):
+        @pl.when(there[side])
+        def _():
+            fn()
 
     def normalise(c):
         for k in (0, 1):
-            v = feat[k, c].astype(jnp.float32)
+            v = feat[k, c - 1].astype(jnp.float32)
             total = jnp.sum(v * v, axis=-1, keepdims=True)
-            own[c + 1, k * PATCH : (k + 1) * PATCH] = (v * lax.rsqrt(total + 1e-06)).astype(
+            own[c, k * PATCH : (k + 1) * PATCH] = (v * lax.rsqrt(total + 1e-06)).astype(
                 jnp.bfloat16
             )
 
-    for c in range(WIDTH):
-        normalise(c)
-
-    def group(step, _):
-        for i in range(WIDTH):
-            normalise(step * WIDTH + i)
-        start_edges(step - 1)
-        return 0
-
-    lax.fori_loop(1, STEPS, group, 0)
-    start_edges(STEPS - 1)
-
-    def side(k):
+    def side_copy(k):
         dr, dc = DIRS[k]
-        device = device_at(row + dr, col + dc)
-        return halo_copy(own, halo, dr, dc, csend.at[k], crecv.at[k], device)
+        return halo_copy(own, halo, dr, dc, csend.at[k], crecv.at[k], device_at(row, col + dc))
 
     def side_mask(k):
         dr, dc = DIRS[k]
-        device = device_at(row + dr, col + dc)
-        return mask_copy(mask, dr, dc, msend.at[k], mrecv.at[k], device)
-
-    for k, (dr, dc) in enumerate(DIRS):
+        return mask_copy(mask, dr, dc, msend.at[k], mrecv.at[k], device_at(row + dr, col + dc))
+
+    for k in range(4):
+        dr, dc = DIRS[k]
 
         @pl.when(inside(row + dr, col + dc))
         def _(k=k):
             side_mask(k).start()
-            if k >= 2:
-                side(k).start()
+
+    half = TC // 2
+    normalise(1)
+    normalise(TC)
+    normalise(2)
+    normalise(TC - 1)
+    for side in (0, 1):
+        on(side, lambda side=side: (tile_copy(side, 1).start(), tile_copy(side, TC).start()))
+    for k in (2, 3):
+
+        @pl.when(inside(row, col + DIRS[k][1]))
+        def _(k=k):
+            side_copy(k).start()
+
+    def group(g, _):
+        normalise(g + 1)
+        normalise(TC - g)
+        on(0, lambda: tile_copy(0, TC + 1 - g).start())
+        on(1, lambda: tile_copy(1, g).start())
+        return 0
+
+    lax.fori_loop(2, half, group, 0)
+    on(0, lambda: tile_copy(0, half + 1).start())
+    on(1, lambda: (tile_copy(1, half).start(), tile_copy(1, half + 1).start()))
 
     lane = lax.broadcasted_iota(jnp.int32, (128, 128), 1)
     sub = lax.broadcasted_iota(jnp.int32, (128, 128), 0)
     diagonal = lane == sub
-    seen = (lane < PATCH) == (sub < PATCH)
-
-    def block(c, cc, other, upper, lower, kind):
-        s = lax.dot_general(own[c], other[cc], NT, preferred_element_type=jnp.float32)
+    first = lane[0:1] < PATCH
+
+    def block(c, cc):
+        s = lax.dot_general(own[c], own[cc], NT, preferred_element_type=jnp.float32)
         w = jnp.exp(AFFINITY_TEMP * (s - 1.0))
-        m = jnp.where(lane[0:1] < PATCH, upper[cc, 0:1], lower[cc, 0:1])
-        keep = jnp.broadcast_to(m, (128, 128)) > 0.5
-        if kind == 1:
-            keep = keep & seen
-        return jnp.where(keep, w, 0.0)
-
-    def own_blocks(c, parts):
+        m = jnp.where(first, mask[0, cc, 0:1], mask[1, cc, 0:1])
+        return jnp.where(jnp.broadcast_to(m, (128, 128)) > 0.5, w, 0.0)
+
+    def own_blocks(c):
         total = jnp.zeros((128, 1), jnp.float32)
-        for d in parts:
-            w = block(c, c + d - 1, own, mask.at[0], mask.at[1], 0)
+        for d in range(3):
+            w = block(c, c + d - 1)
             total = total + jnp.sum(w, axis=1, keepdims=True)
             if d == 1:
                 self_w = jnp.sum(jnp.where(diagonal, w, 0.0), axis=1, keepdims=True)
                 diag_ref[c - 1] = jnp.broadcast_to(self_w, (128, 128))
                 w = jnp.where(diagonal, 0.0, w)
-            e_ref[c - 1, 0, :, d * 128 : (d + 1) * 128] = w.astype(jnp.bfloat16)
-        return total
-
-    def halo_blocks(c):
-        total = jnp.zeros((128, 1), jnp.float32)
-        for d in range(3):
-            w = block(c, c + d - 1, halo, mask.at[2], mask.at[3], 1)
-            total = total + jnp.sum(w, axis=1, keepdims=True)
-            e_ref[c - 1, 1, :, d * 128 : (d + 1) * 128] = w.astype(jnp.bfloat16)
-        return total
-
-    def inner(c, _):
-        deg[c] = jnp.broadcast_to(own_blocks(c, (0, 1, 2)), (128, 128))
-        return 0
+            e_ref[c - 1, :, d * 128 : (d + 1) * 128] = w.astype(jnp.bfloat16)
+        deg[c] = jnp.broadcast_to(total, (128, 128))
 
     meanwhile()
-    lax.fori_loop(2, TC, inner, 0, unroll=2)
-
-    for k, (dr, dc) in enumerate(DIRS):
+
+    for k in range(4):
+        dr, dc = DIRS[k]
 
         @pl.when(inside(row - dr, col - dc))
         def _(k=k):
             side_mask(k).wait_recv()
             if k >= 2:
-                side(k).wait_recv()
-
+                side_copy(k).wait_recv()
+
+    def rows_of(left, right, right_mask, c):
+        s = lax.dot_general(left, right, NT, preferred_element_type=jnp.float32)
+        w = jnp.exp(AFFINITY_TEMP * (s - 1.0))
+        m0 = jnp.where(first, mask[right_mask, c - 1, 0:1], mask[right_mask, c, 0:1])
+        m1 = mask[right_mask, c + 1, 0:1]
+        w0 = jnp.where(jnp.broadcast_to(m0, (PATCH, 128)) > 0.5, w[:, :128], 0.0)
+        w1 = jnp.where(jnp.broadcast_to(m1[:, :PATCH], (PATCH, PATCH)) > 0.5, w[:, 128:], 0.0)
+        w1 = jnp.concatenate([w1, jnp.zeros((PATCH, PATCH), jnp.float32)], axis=1)
+        return jnp.concatenate([w0, w1], axis=1).astype(jnp.bfloat16)
+
+    def near(ref, side, c):
+        return ref[pl.ds(c - 1, 3), side * PATCH : (side + 1) * PATCH].reshape(3 * PATCH, -1)
+
+    def serve(side, c):
+        tile_arrival(side, c).wait_recv()
+        left = halo[c, side * PATCH : (side + 1) * PATCH]
+        served[side, c - 1] = rows_of(left, near(own, side, c), side, c)
+        weights_copy(side, c).start()
+
+    def at_home(side, c):
+        left = own[c, side * PATCH : (side + 1) * PATCH]
+        eh_ref[side, c - 1] = rows_of(left, near(halo, side, c), 2 + side, c)
+
+    def inner(c, _):
+        own_blocks(c)
+        return 0
+
+    lax.fori_loop(1, 4, inner, 0)
     for c in (1, TC):
-        deg[c] = jnp.broadcast_to(own_blocks(c, (0, 1, 2)), (128, 128))
+        for side in (0, 1):
+            on(side, lambda side=side, c=c: serve(side, c))
+    lax.fori_loop(4, 6, inner, 0)
+    on(0, lambda: serve(0, 2))
+    on(1, lambda: serve(1, TC - 1))
+
+    def arrive(g, _):
+        on(0, lambda: (serve(0, g + 1), at_home(0, g)))
+        on(1, lambda: (serve(1, TC - g), at_home(1, TC + 1 - g)))
+
+        @pl.when(g < 7)
+        def _():
+            own_blocks(2 * g + 2)
+            own_blocks(2 * g + 3)
+
+        @pl.when(g == 7)
+        def _():
+            own_blocks(TC)
+
+        return 0
+
+    lax.fori_loop(2, half, arrive, 0)
+    on(0, lambda: (serve(0, half + 1), at_home(0, half)))
 
     def finish(c):
-        total = deg[c][:, 0:1] + halo_blocks(c)
-        m = jnp.where(lane[0:1] < PATCH, mask[0, c, 0:1], mask[1, c, 0:1])
+        eh = jnp.concatenate([eh_ref[0, c - 1], eh_ref[1, c - 1]], axis=0).astype(jnp.float32)
+        total = deg[c][:, 0:1] + jnp.sum(eh, axis=1, keepdims=True)
+        m = jnp.where(first, mask[0, c, 0:1], mask[1, c, 0:1])
         mine = jnp.sum(jnp.where(diagonal, jnp.broadcast_to(m, (128, 128)), 0.0), axis=1, keepdims=True)
         scale = lax.rsqrt(1.0 + mine * total)
         self_w = diag_ref[c - 1]
@@ -240,44 +316,41 @@
         mine_ref[c - 1] = jnp.broadcast_to(scale * mine, (128, 128))
         diag_ref[c - 1] = 1.0 + (mine * scale * scale) * self_w
 
-    def wait_edges(step):
-        def go(k, copy):
-            @pl.when(inside(row - DIRS[k][0], col))
-            def _():
-                copy.wait_recv()
-
-        edges(step, go)
-
-    wait_edges(0)
-    for c in range(1, WIDTH):
+    def back(side, columns):
+        for c in columns:
+            weights_arrival(side, c).wait_recv()
+
+    up = [1] + list(range(half + 1, TC + 1))
+    down = list(range(1, half + 2)) + [TC]
+    on(0, lambda: back(0, up))
+    on(1, lambda: back(1, down))
+
+    def finish_one(c, _):
         finish(c)
-
-    def halo_group(step, _):
-        wait_edges(step)
-        for i in range(WIDTH):
-            finish(step * WIDTH + i)
-        return 0
-
-    lax.fori_loop(1, STEPS, halo_group, 0)
-    finish(TC)
-
-    def drain(step, _):
-        def go(k, copy):
-            @pl.when(inside(row + DIRS[k][0], col))
-            def _():
-                copy.wait_send()
-
-        edges(step, go)
-        return 0
-
-    lax.fori_loop(0, STEPS, drain, 0)
-    for k, (dr, dc) in enumerate(DIRS):
-
-        @pl.when(inside(row + dr, col + dc))
-        def _(k=k):
-            side_mask(k).wait_send()
-            if k >= 2:
-                side(k).wait_send()
+        return 0
+
+    lax.fori_loop(1, TC + 1, finish_one, 0, unroll=4)
+
+    def sent():
+        for side, mine, theirs in ((0, up, down), (1, down, up)):
+
+            def go(side=side, mine=mine, theirs=theirs):
+                for c in mine:
+                    tile_copy(side, c).wait_send()
+                for c in theirs:
+                    weights_copy(side, c).wait_send()
+
+            on(side, go)
+        for k in range(4):
+            dr, dc = DIRS[k]
+
+            @pl.when(inside(row + dr, col + dc))
+            def _(k=k):
+                side_mask(k).wait_send()
+                if k >= 2:
+                    side_copy(k).wait_send()
+
+    return sent
 
 
 def stage_peers(pos):
@@ -312,9 +385,9 @@
 
 def kernel(
     feat, tissue, probe, out_ref,
-    ufeat, hfeat, mask, deg, e_ref, scale_ref, mine_ref, diag_ref,
+    ufeat, hfeat, mask, deg, served, e_ref, eh_ref, scale_ref, mine_ref, diag_ref,
     own, halo, acc, y, pair, total, gsum,
-    usend, urecv, csend, crecv, msend, mrecv, psend, precv, gsend, grecv,
+    fsend, frecv, csend, crecv, msend, mrecv, rsend, rrecv, psend, precv, gsend, grecv,
 ):
     pos = position()
     row, col = row_col(pos)
@@ -327,10 +400,11 @@
         own[i, TC + 1] = zero
 
         def one(c, _):
-            halo[i, c] = zero
+            for side in (0, 1):
+                halo[i, side, c] = zero[:PATCH]
             return 0
 
-        lax.fori_loop(0, TC + 2, one, 0, unroll=6)
+        lax.fori_loop(0, TC + 3, one, 0)
         return 0
 
     lax.fori_loop(0, ITERS, clear, 0)
@@ -347,16 +421,23 @@
 
         lax.fori_loop(0, TC, load, 0, unroll=4)
 
-    affinity(
-        row, col, feat, tissue, e_ref, scale_ref, mine_ref, diag_ref, ufeat, hfeat, mask, deg,
-        usend, urecv, csend, crecv, msend, mrecv, ready, meanwhile,
+    sent = affinity(
+        row, col, feat, tissue, e_ref, eh_ref, scale_ref, mine_ref, diag_ref, ufeat, hfeat, mask,
+        deg, served, fsend, frecv, csend, crecv, msend, mrecv, rsend, rrecv, ready, meanwhile,
     )
 
     def panel(t, k):
         dr, dc = DIRS[k]
-        return halo_copy(
-            own.at[t], halo.at[t], dr, dc, psend.at[t, k], precv.at[t, k],
-            device_at(row + dr, col + dc),
+        src, dst = send_slices(dr, dc)
+        if dr == 0:
+            a, b = own.at[t, src], own.at[t, dst]
+        elif dr < 0:
+            a, b = own.at[t, src, 0:PATCH], halo.at[t, 1, dst]
+        else:
+            a, b = own.at[t, src, PATCH : 2 * PATCH], halo.at[t, 0, dst]
+        return pltpu.make_async_remote_copy(
+            src_ref=a, dst_ref=b, send_sem=psend.at[t, k], recv_sem=precv.at[t, k],
+            device_id=device_at(row + dr, col + dc), device_id_type=MESH_ID,
         )
 
     def each_target(fn):
@@ -376,14 +457,21 @@
     def own_part(t, first, stop):
         def go(c, _):
             b = own[t, pl.ds(c, 3)].reshape(384, 128)
-            acc[c] = jnp.dot(e_ref[c, 0], b, preferred_element_type=jnp.float32)
+            acc[c] = jnp.dot(e_ref[c], b, preferred_element_type=jnp.float32)
             return 0
 
         lax.fori_loop(first, stop, go, 0, unroll=stop - first)
 
     def product(t, c):
-        b = halo[t, pl.ds(c, 3)].reshape(384, 128)
-        v = acc[c] + jnp.dot(e_ref[c, 1], b, preferred_element_type=jnp.float32)
+        v = [
+            jnp.dot(
+                eh_ref[side, c],
+                halo[t, side, pl.ds(c, 4)].reshape(256, 128),
+                preferred_element_type=jnp.float32,
+            )
+            for side in (0, 1)
+        ]
+        v = acc[c] + jnp.concatenate(v, axis=0)
         v = v + pltpu.roll(v, RANK, 1)
         return y[c] * diag_ref[c] + mine_ref[c] * v
 
@@ -506,6 +594,7 @@
 
     lax.fori_loop(0, TC, last, 0, unroll=4)
 
+    sent()
     for t in range(ITERS):
         each_target(lambda k: panel(t, k).wait_send())
         for s, (place, peers) in enumerate(stages):
@@ -539,18 +628,21 @@
             pltpu.VMEM(wide, jnp.bfloat16),
             pltpu.VMEM((4, TC + 2, 8, 128), jnp.float32),
             pltpu.VMEM((TC + 1, 128, 128), jnp.float32),
-            pltpu.VMEM((TC, 2, 128, 384), jnp.bfloat16),
+            pltpu.VMEM((2, TC, PATCH, 256), jnp.bfloat16),
+            pltpu.VMEM((TC, 128, 384), jnp.bfloat16),
+            pltpu.VMEM((2, TC, PATCH, 256), jnp.bfloat16),
             pltpu.VMEM(full, jnp.float32),
             pltpu.VMEM(full, jnp.float32),
             pltpu.VMEM(full, jnp.float32),
             pltpu.VMEM((ITERS, TC + 2, 128, 128), jnp.bfloat16),
-            pltpu.VMEM((ITERS, TC + 2, 128, 128), jnp.bfloat16),
+            pltpu.VMEM((ITERS, 2, TC + 3, PATCH, 128), jnp.bfloat16),
             pltpu.VMEM(full, jnp.float32),
             pltpu.VMEM(full, jnp.float32),
             pltpu.VMEM(full, jnp.bfloat16),
             pltpu.VMEM((128, 128), jnp.float32),
             pltpu.VMEM((ITERS, 4, 4, 32, 128), jnp.float32),
-            DMA((2, STEPS)), DMA((2, STEPS)), DMA((8,)), DMA((8,)), DMA((8,)), DMA((8,)),
+            DMA((2, TC + 1)), DMA((2, TC + 1)), DMA((4,)), DMA((4,)), DMA((4,)), DMA((4,)),
+            DMA((2, TC + 1)), DMA((2, TC + 1)),
             DMA((ITERS, 8)), DMA((ITERS, 8)), DMA((ITERS, 4, 3)), DMA((ITERS, 4, 3)),
         ],
         compiler_params=pltpu.CompilerParams(

time: 159 us -> 149 us (0.937)
  Pallas kernels: 154 us -> 144 us
    pallas_call x1, Pallas kernels: 154 us -> 144 us  [local(): pl.pallas_call(kernel, out_shape=jax.ShapeDtypeStruct((2, TC, PATCH, RANK...]
where the time goes in v3:
time: 149 us
  Pallas kernels  144 us (97%)
  local copies, waits for them, and re-layouts  4.83 us (3%)
    pallas_call x1, Pallas kernels, local(): pl.pallas_call(kernel, out_shape=jax.ShapeDtypeStruct((2, TC, PATCH, RANK...  144 us

profile of v3, /device:TPU:0, one launch (start us, length us, event | category | flops | bytes accessed | tf_op | source)
XLA Modules:
  0.0 149.0 jit_solution(17245681203820446488)
XLA Ops:
  0.0 2.5 %reshape.6.probe = f32[2,16,64,64]{3,2,1,0:T(8,128)} reshape(f32[2,16,4096]{2,1,0:T(8,128)} %param.5) | data formatting | bytes 1048576 | tf_op jit(solution)/shard_map/reshape | solution.py:652
  2.5 144.1 %range_finder.1 = f32[2,16,64,64]{3,2,1,0:T(8,128)} custom-call(bf16[2,16,64,1024]{3,2,1,0:T(8,128)(2,1)} %feat.1, s32[2,16,64]{2,1,0:T(8,128)} %tissue.1, f32[2,16,64,64]{3,2,1,0:T(8,128)} %reshape.6.probe), custom_call_target="tpu_custom_call" | custom-call | tf_op jit(solution)/shard_map/range_finder/pallas_call | solution.py:621
  146.6 2.4 %reshape.7 = f32[2,16,4096]{2,1,0:T(8,128)} reshape(f32[2,16,64,64]{3,2,1,0:T(8,128)} %range_finder.1) | data formatting | bytes 1048576 | tf_op jit(solution)/shard_map/reshape | solution.py:653

commit v4 on v3

--- a/solution.py
+++ b/solution.py
@@ -19,6 +19,7 @@
 TC = 16
 MESH_ID = pl.DeviceIdType.MESH
 AFFINITY_TEMP = 4.0
+LATE = 6
 
 DIRS = ((-1, 0), (1, 0), (0, -1), (0, 1), (-1, -1), (-1, 1), (1, -1), (1, 1))
 
@@ -166,8 +167,16 @@
             device_id_type=MESH_ID,
         )
 
+    crossing = (row == 3) | (row == 4)
+    yields = [row == 4, row == 3]
+
     def on(side, fn):
         @pl.when(there[side])
+        def _():
+            fn()
+
+    def early(side, fn):
+        @pl.when(there[side] & jnp.logical_not(yields[side]))
         def _():
             fn()
 
@@ -198,25 +207,40 @@
     normalise(1)
     normalise(TC)
     normalise(2)
-    normalise(TC - 1)
-    for side in (0, 1):
-        on(side, lambda side=side: (tile_copy(side, 1).start(), tile_copy(side, TC).start()))
     for k in (2, 3):
 
         @pl.when(inside(row, col + DIRS[k][1]))
         def _(k=k):
             side_copy(k).start()
 
+    normalise(TC - 1)
+    for side in (0, 1):
+        early(side, lambda side=side: (tile_copy(side, 1).start(), tile_copy(side, TC).start()))
+
     def group(g, _):
         normalise(g + 1)
         normalise(TC - g)
-        on(0, lambda: tile_copy(0, TC + 1 - g).start())
-        on(1, lambda: tile_copy(1, g).start())
+        early(0, lambda: tile_copy(0, TC + 1 - g).start())
+        early(1, lambda: tile_copy(1, g).start())
         return 0
 
     lax.fori_loop(2, half, group, 0)
-    on(0, lambda: tile_copy(0, half + 1).start())
-    on(1, lambda: (tile_copy(1, half).start(), tile_copy(1, half + 1).start()))
+    early(0, lambda: tile_copy(0, half + 1).start())
+    early(1, lambda: (tile_copy(1, half).start(), tile_copy(1, half + 1).start()))
+
+    def arrived(k, fn):
+        dr, dc = DIRS[k]
+
+        @pl.when(inside(row - dr, col - dc))
+        def _():
+            fn()
+
+    def sides():
+        for k in (2, 3):
+            arrived(k, lambda k=k: (side_mask(k).wait_recv(), side_copy(k).wait_recv()))
+
+    up = [1] + list(range(TC, half, -1))
+    down = [TC] + list(range(1, half + 2))
 
     lane = lax.broadcasted_iota(jnp.int32, (128, 128), 1)
     sub = lax.broadcasted_iota(jnp.int32, (128, 128), 0)
@@ -243,15 +267,6 @@
 
     meanwhile()
 
-    for k in range(4):
-        dr, dc = DIRS[k]
-
-        @pl.when(inside(row - dr, col - dc))
-        def _(k=k):
-            side_mask(k).wait_recv()
-            if k >= 2:
-                side_copy(k).wait_recv()
-
     def rows_of(left, right, right_mask, c):
         s = lax.dot_general(left, right, NT, preferred_element_type=jnp.float32)
         w = jnp.exp(AFFINITY_TEMP * (s - 1.0))
@@ -265,8 +280,9 @@
     def near(ref, side, c):
         return ref[pl.ds(c - 1, 3), side * PATCH : (side + 1) * PATCH].reshape(3 * PATCH, -1)
 
-    def serve(side, c):
-        tile_arrival(side, c).wait_recv()
+    def serve(side, c, wait=True):
+        if wait:
+            tile_arrival(side, c).wait_recv()
         left = halo[c, side * PATCH : (side + 1) * PATCH]
         served[side, c - 1] = rows_of(left, near(own, side, c), side, c)
         weights_copy(side, c).start()
@@ -279,17 +295,44 @@
         own_blocks(c)
         return 0
 
-    lax.fori_loop(1, 4, inner, 0)
-    for c in (1, TC):
-        for side in (0, 1):
-            on(side, lambda side=side, c=c: serve(side, c))
-    lax.fori_loop(4, 6, inner, 0)
+    lax.fori_loop(2, 6, inner, 0)
+    @pl.when(crossing)
+    def _():
+        sides()
+
+    for side, columns in ((0, up), (1, down)):
+
+        @pl.when(yields[side])
+        def _(side=side, columns=columns):
+            for c in columns:
+                tile_copy(side, c).start()
+
+    for k in (0, 1):
+        arrived(k, lambda k=k: side_mask(k).wait_recv())
     on(0, lambda: serve(0, 2))
     on(1, lambda: serve(1, TC - 1))
 
     def arrive(g, _):
-        on(0, lambda: (serve(0, g + 1), at_home(0, g)))
-        on(1, lambda: (serve(1, TC - g), at_home(1, TC + 1 - g)))
+        on(0, lambda: serve(0, g + 1))
+        on(1, lambda: serve(1, TC - g))
+
+        @pl.when(g == LATE)
+        def _():
+            @pl.when(jnp.logical_not(crossing))
+            def _():
+                sides()
+
+            for c in (1, TC):
+                for side in (0, 1):
+                    on(side, lambda side=side, c=c: serve(side, c, c != (1, TC)[side]))
+
+        @pl.when(g == 2)
+        def _():
+            for side in (0, 1):
+                on(side, lambda side=side: (tile_arrival(side, (1, TC)[side]).wait_recv()))
+
+        on(0, lambda: at_home(0, g))
+        on(1, lambda: at_home(1, TC + 1 - g))
 
         @pl.when(g < 7)
         def _():
@@ -298,6 +341,7 @@
 
         @pl.when(g == 7)
         def _():
+            own_blocks(1)
             own_blocks(TC)
 
         return 0
@@ -320,8 +364,6 @@
         for c in columns:
             weights_arrival(side, c).wait_recv()
 
-    up = [1] + list(range(half + 1, TC + 1))
-    down = list(range(1, half + 2)) + [TC]
     on(0, lambda: back(0, up))
     on(1, lambda: back(1, down))
 

time: 149 us -> 137 us (0.919)
  Pallas kernels: 144 us -> 132 us
    pallas_call x1, Pallas kernels: 144 us -> 132 us  [local(): pl.pallas_call(kernel, out_shape=jax.ShapeDtypeStruct((2, TC, PATCH, RANK...]
where the time goes in v4:
time: 137 us
  Pallas kernels  132 us (96%)
  local copies, waits for them, and re-layouts  4.83 us (4%)
    pallas_call x1, Pallas kernels, local(): pl.pallas_call(kernel, out_shape=jax.ShapeDtypeStruct((2, TC, PATCH, RANK...  132 us

profile of v4, /device:TPU:0, one launch (start us, length us, event | category | flops | bytes accessed | tf_op | source)
XLA Modules:
  0.0 137.3 jit_solution(17096131284948822286)
XLA Ops:
  0.0 2.5 %reshape.6.probe = f32[2,16,64,64]{3,2,1,0:T(8,128)} reshape(f32[2,16,4096]{2,1,0:T(8,128)} %param.5) | data formatting | bytes 1048576 | tf_op jit(solution)/shard_map/reshape | solution.py:694
  2.5 132.4 %range_finder.1 = f32[2,16,64,64]{3,2,1,0:T(8,128)} custom-call(bf16[2,16,64,1024]{3,2,1,0:T(8,128)(2,1)} %feat.1, s32[2,16,64]{2,1,0:T(8,128)} %tissue.1, f32[2,16,64,64]{3,2,1,0:T(8,128)} %reshape.6.probe), custom_call_target="tpu_custom_call" | custom-call | tf_op jit(solution)/shard_map/range_finder/pallas_call | solution.py:663
  134.9 2.4 %reshape.7 = f32[2,16,4096]{2,1,0:T(8,128)} reshape(f32[2,16,64,64]{3,2,1,0:T(8,128)} %range_finder.1) | data formatting | bytes 1048576 | tf_op jit(solution)/shard_map/reshape | solution.py:695

commit v5 on v4

--- a/solution.py
+++ b/solution.py
@@ -19,7 +19,6 @@
 TC = 16
 MESH_ID = pl.DeviceIdType.MESH
 AFFINITY_TEMP = 4.0
-LATE = 6
 
 DIRS = ((-1, 0), (1, 0), (0, -1), (0, 1), (-1, -1), (-1, 1), (1, -1), (1, 1))
 
@@ -104,7 +103,7 @@
 
 def affinity(
     row, col, feat, tissue, e_ref, eh_ref, scale_ref, mine_ref, diag_ref, own, halo, mask, deg, served,
-    fsend, frecv, csend, crecv, msend, mrecv, rsend, rrecv, ready, meanwhile,
+    fsend, frecv, csend, crecv, msend, mrecv, rsend, rrecv, ready, meanwhile, load_feat,
 ):
     for k in (2, 3):
         mask[k] = jnp.zeros((TC + 2, 8, 128), jnp.float32)
@@ -181,6 +180,7 @@
             fn()
 
     def normalise(c):
+        load_feat(c).wait()
         for k in (0, 1):
             v = feat[k, c - 1].astype(jnp.float32)
             total = jnp.sum(v * v, axis=-1, keepdims=True)
@@ -316,16 +316,6 @@
         on(0, lambda: serve(0, g + 1))
         on(1, lambda: serve(1, TC - g))
 
-        @pl.when(g == LATE)
-        def _():
-            @pl.when(jnp.logical_not(crossing))
-            def _():
-                sides()
-
-            for c in (1, TC):
-                for side in (0, 1):
-                    on(side, lambda side=side, c=c: serve(side, c, c != (1, TC)[side]))
-
         @pl.when(g == 2)
         def _():
             for side in (0, 1):
@@ -339,15 +329,20 @@
             own_blocks(2 * g + 2)
             own_blocks(2 * g + 3)
 
-        @pl.when(g == 7)
-        def _():
-            own_blocks(1)
-            own_blocks(TC)
-
         return 0
 
     lax.fori_loop(2, half, arrive, 0)
     on(0, lambda: (serve(0, half + 1), at_home(0, half)))
+
+    @pl.when(jnp.logical_not(crossing))
+    def _():
+        sides()
+
+    for c in (1, TC):
+        for side in (0, 1):
+            on(side, lambda side=side, c=c: serve(side, c, c != (1, TC)[side]))
+    for c in (1, TC):
+        own_blocks(c)
 
     def finish(c):
         eh = jnp.concatenate([eh_ref[0, c - 1], eh_ref[1, c - 1]], axis=0).astype(jnp.float32)
@@ -407,15 +402,33 @@
 
 def inverse_factor(gram):
     n = RANK
-    m = jnp.concatenate([gram, jnp.where(eye(n), 1.0, 0.0)], axis=1)
-    sub = lax.broadcasted_iota(jnp.int32, (n, 2 * n), 0)
-    lane = lax.broadcasted_iota(jnp.int32, (n, 2 * n), 1)
-    for k in range(n - 1):
-        column = jnp.broadcast_to(m[:, k : k + 1], (n, 2 * n))
-        pivot = column[k : k + 1, :]
-        line = m[k : k + 1, :] / pivot
-        m = m - jnp.where(sub > k, column, 0.0) * line
-    d = jnp.sum(jnp.where(lane == sub, m, 0.0), axis=1, keepdims=True)
+    row_block = 8
+    on_diagonal = jnp.where(eye(n), gram, 0.0)
+    by_row = lax.rsqrt(jnp.sum(on_diagonal, axis=1, keepdims=True))
+    by_lane = lax.rsqrt(jnp.sum(on_diagonal, axis=0, keepdims=True))
+    start = jnp.concatenate([gram * by_row * by_lane, jnp.where(eye(n), by_lane, 0.0)], axis=1)
+    m = [start[q : q + row_block] for q in range(0, n, row_block)]
+    sub = lax.broadcasted_iota(jnp.int32, (row_block, 2 * n), 0)
+    for k in range(0, n, 2):
+        j, i = divmod(k, row_block)
+        left = [jnp.broadcast_to(m[q][:, k : k + 1], (row_block, 2 * n)) for q in range(j, len(m))]
+        right = [
+            jnp.broadcast_to(m[q][:, k + 1 : k + 2], (row_block, 2 * n)) for q in range(j, len(m))
+        ]
+        r0, r1 = m[j][i : i + 1], m[j][i + 1 : i + 2]
+        a, b, d = left[0][i : i + 1], left[0][i + 1 : i + 2], right[0][i + 1 : i + 2]
+        inv = 1.0 / (a * d - b * b)
+        u0 = (d * r0 - b * r1) * inv
+        u1 = (a * r1 - b * r0) * inv
+        second = r1 - (b / a) * r0
+        for q in range(j, len(m)):
+            new = m[q] - (left[q - j] * u0 + right[q - j] * u1)
+            if q == j:
+                new = jnp.where(sub > i + 1, new, m[q])
+                new = jnp.where(sub == i + 1, second, new)
+            m[q] = new
+    m = jnp.concatenate(m, axis=0)
+    d = jnp.sum(jnp.where(eye(n), m[:, :n], 0.0), axis=1, keepdims=True)
     return m[:, n:] * lax.rsqrt(d)
 
 
@@ -426,15 +439,25 @@
 
 
 def kernel(
-    feat, tissue, probe, out_ref,
-    ufeat, hfeat, mask, deg, served, e_ref, eh_ref, scale_ref, mine_ref, diag_ref,
+    feat_hbm, tissue, probe, out_ref,
+    feat, ufeat, hfeat, mask, deg, served, e_ref, eh_ref, scale_ref, mine_ref, diag_ref,
     own, halo, acc, y, pair, total, gsum,
-    fsend, frecv, csend, crecv, msend, mrecv, rsend, rrecv, psend, precv, gsend, grecv,
+    fsend, frecv, csend, crecv, msend, mrecv, rsend, rrecv, psend, precv, gsend, grecv, isem,
 ):
+    def load_feat(c):
+        return pltpu.make_async_copy(
+            feat_hbm.at[:, pl.ds(c - 1, 1)], feat.at[:, pl.ds(c - 1, 1)], isem.at[c]
+        )
+
+    for c in range(1, TC // 2 + 1):
+        load_feat(c).start()
+        load_feat(TC + 1 - c).start()
+
     pos = position()
     row, col = row_col(pos)
     stages = stage_peers(pos)
     low = lax.broadcasted_iota(jnp.int32, (128, 128), 1) < RANK
+    lane_low = lax.broadcasted_iota(jnp.int32, (PATCH, 128), 1) < RANK
     zero = jnp.zeros((128, 128), jnp.bfloat16)
 
     def clear(i, _):
@@ -458,14 +481,17 @@
         def load(c, _):
             for k in (0, 1):
                 v = probe[k, c]
-                y[c, k * PATCH : (k + 1) * PATCH] = jnp.concatenate([v, v], axis=1)
+                w = pltpu.roll(v, RANK, 1)
+                even = lane_low[: PATCH // 2]
+                y[c, pl.ds(k * PATCH, PATCH // 2, stride=2)] = jnp.where(even, v, w)
+                y[c, pl.ds(k * PATCH + 1, PATCH // 2, stride=2)] = jnp.where(even, w, v)
             return 0
 
         lax.fori_loop(0, TC, load, 0, unroll=4)
 
     sent = affinity(
         row, col, feat, tissue, e_ref, eh_ref, scale_ref, mine_ref, diag_ref, ufeat, hfeat, mask,
-        deg, served, fsend, frecv, csend, crecv, msend, mrecv, rsend, rrecv, ready, meanwhile,
+        deg, served, fsend, frecv, csend, crecv, msend, mrecv, rsend, rrecv, ready, meanwhile, load_feat,
     )
 
     def panel(t, k):
@@ -629,9 +655,11 @@
     factor = math.sqrt(float(NROW * 2 * NCOL * TC * PATCH))
 
     def last(c, _):
-        v = factor * solve(pair[c])
+        y[c] = factor * solve(pair[c])
         for k in (0, 1):
-            out_ref[k, c] = v[k * PATCH : (k + 1) * PATCH, :RANK]
+            even = y[c, pl.ds(k * PATCH, PATCH // 2, stride=2)]
+            odd = y[c, pl.ds(k * PATCH + 1, PATCH // 2, stride=2)]
+            out_ref[k, c] = jnp.where(lane_low[: PATCH // 2], even, odd)
         return 0
 
     lax.fori_loop(0, TC, last, 0, unroll=4)
@@ -662,10 +690,11 @@
     wide = (TC + 2, 128, width)
     out = pl.pallas_call(
         kernel,
-        out_shape=jax.ShapeDtypeStruct((2, TC, PATCH, RANK), jnp.float32),
-        in_specs=[VM] * 3,
+        out_shape=jax.ShapeDtypeStruct((2, TC, PATCH // 2, 2 * RANK), jnp.float32),
+        in_specs=[pl.BlockSpec(memory_space=pl.ANY), VM, VM],
         out_specs=VM,
         scratch_shapes=[
+            pltpu.VMEM(features.shape, jnp.bfloat16),
             pltpu.VMEM(wide, jnp.bfloat16),
             pltpu.VMEM(wide, jnp.bfloat16),
             pltpu.VMEM((4, TC + 2, 8, 128), jnp.float32),
@@ -686,12 +715,13 @@
             DMA((2, TC + 1)), DMA((2, TC + 1)), DMA((4,)), DMA((4,)), DMA((4,)), DMA((4,)),
             DMA((2, TC + 1)), DMA((2, TC + 1)),
             DMA((ITERS, 8)), DMA((ITERS, 8)), DMA((ITERS, 4, 3)), DMA((ITERS, 4, 3)),
+            DMA((TC + 1,)),
         ],
         compiler_params=pltpu.CompilerParams(
             collective_id=0, has_side_effects=True, vmem_limit_bytes=LIMIT
         ),
         name="range_finder",
-    )(features, tissue, probe.reshape(2, TC, PATCH, RANK))
+    )(features, tissue, probe.reshape(2, TC, PATCH // 2, 2 * RANK))
     return out.reshape(2, TC, PATCH * RANK)
 
 

time: 137 us -> 128 us (0.934)
  Pallas kernels: 132 us -> 124 us
    pallas_call x1, Pallas kernels: 132 us -> 124 us  [local(): pl.pallas_call(kernel, out_shape=jax.ShapeDtypeStruct((2, TC, PATCH // 2,...]
    reshape x1 -> x0, local copies, waits for them, and re-layouts: 2.45 us -> none  [local(): probe.reshape(2, TC, PATCH, RANK)]
    unnamed x0 -> x1, local copies, waits for them, and re-layouts: none -> 1.93 us
where the time goes in v5:
time: 128 us
  Pallas kernels  124 us (97%)
  local copies, waits for them, and re-layouts  3.86 us (3%)
    pallas_call x1, Pallas kernels, local(): pl.pallas_call(kernel, out_shape=jax.ShapeDtypeStruct((2, TC, PATCH // 2,...  124 us

profile of v5, /device:TPU:0, one launch (start us, length us, event | category | flops | bytes accessed | tf_op | source)
XLA Modules:
  0.0 127.9 jit_solution(9743508420416082963)
XLA Ops:
  0.0 1.9 %copy.4 = f32[4,8,32,128]{3,2,1,0:T(8,128)} copy(f32[4,8,32,128]{3,1,2,0:T(8,128)} %bitcast.7) | data formatting | bytes 1048576
  1.9 124.0 %range_finder.1 = f32[2,16,32,128]{3,2,1,0:T(8,128)} custom-call(bf16[2,16,64,1024]{3,2,1,0:T(8,128)(2,1)} %feat_hbm.1, s32[2,16,64]{2,1,0:T(8,128)} %tissue.1, f32[2,16,32,128]{3,2,1,0:T(8,128)} %bitcast.6), custom_call_target="tpu_custom_call" | custom-call | tf_op jit(solution)/shard_map/range_finder/pallas_call | solution.py:691
  125.9 1.9 %reshape.7 = f32[2,16,4096]{2,1,0:T(8,128)} reshape(f32[2,16,32,128]{3,2,1,0:T(8,128)} %range_finder.1) | data formatting | bytes 1048576 | tf_op jit(solution)/shard_map/reshape | solution.py:725

commit v6 on v5

--- a/solution.py
+++ b/solution.py
@@ -103,7 +103,7 @@
 
 def affinity(
     row, col, feat, tissue, e_ref, eh_ref, scale_ref, mine_ref, diag_ref, own, halo, mask, deg, served,
-    fsend, frecv, csend, crecv, msend, mrecv, rsend, rrecv, ready, meanwhile, load_feat,
+    fsend, frecv, csend, crecv, msend, mrecv, rsend, rrecv, ready, meanwhile, load_feat, then,
 ):
     for k in (2, 3):
         mask[k] = jnp.zeros((TC + 2, 8, 128), jnp.float32)
@@ -312,6 +312,20 @@
     on(0, lambda: serve(0, 2))
     on(1, lambda: serve(1, TC - 1))
 
+    near_end = (row == 0) | (row == NROW - 1)
+    late = near_end & ((col % 4 == 1) | (col % 4 == 2))
+
+    def with_sides():
+        @pl.when(jnp.logical_not(crossing))
+        def _():
+            sides()
+
+        for c in (1, TC):
+            for side in (0, 1):
+                on(side, lambda side=side, c=c: serve(side, c, c != (1, TC)[side]))
+        for c in (1, TC):
+            own_blocks(c)
+
     def arrive(g, _):
         on(0, lambda: serve(0, g + 1))
         on(1, lambda: serve(1, TC - g))
@@ -324,6 +338,10 @@
         on(0, lambda: at_home(0, g))
         on(1, lambda: at_home(1, TC + 1 - g))
 
+        @pl.when((g == 5) & jnp.logical_not(late))
+        def _():
+            with_sides()
+
         @pl.when(g < 7)
         def _():
             own_blocks(2 * g + 2)
@@ -334,15 +352,9 @@
     lax.fori_loop(2, half, arrive, 0)
     on(0, lambda: (serve(0, half + 1), at_home(0, half)))
 
-    @pl.when(jnp.logical_not(crossing))
+    @pl.when(late)
     def _():
-        sides()
-
-    for c in (1, TC):
-        for side in (0, 1):
-            on(side, lambda side=side, c=c: serve(side, c, c != (1, TC)[side]))
-    for c in (1, TC):
-        own_blocks(c)
+        with_sides()
 
     def finish(c):
         eh = jnp.concatenate([eh_ref[0, c - 1], eh_ref[1, c - 1]], axis=0).astype(jnp.float32)
@@ -364,6 +376,7 @@
 
     def finish_one(c, _):
         finish(c)
+        then(c)
         return 0
 
     lax.fori_loop(1, TC + 1, finish_one, 0, unroll=4)
@@ -397,7 +410,7 @@
     y = (pos[2], [(pos[0], pos[1], (pos[2] + d) % 4, pos[3], pos[4]) for d in (1, 2, 3)])
     along = [(z + d) % 4 for d in (1, 2, 3)]
     zz = (z, [(q % 2, pos[1], pos[2], q // 2, pos[4]) for q in along])
-    return [core, y, zz, x]
+    return [core, y, x, zz]
 
 
 def inverse_factor(gram):
@@ -441,7 +454,7 @@
 def kernel(
     feat_hbm, tissue, probe, out_ref,
     feat, ufeat, hfeat, mask, deg, served, e_ref, eh_ref, scale_ref, mine_ref, diag_ref,
-    own, halo, acc, y, pair, total, gsum,
+    own, halo, acc, y, pair, gsum,
     fsend, frecv, csend, crecv, msend, mrecv, rsend, rrecv, psend, precv, gsend, grecv, isem,
 ):
     def load_feat(c):
@@ -489,9 +502,12 @@
 
         lax.fori_loop(0, TC, load, 0, unroll=4)
 
+    def then(c):
+        own[0, c] = pair_of(y[c - 1] * scale_ref[c - 1], low)
+
     sent = affinity(
         row, col, feat, tissue, e_ref, eh_ref, scale_ref, mine_ref, diag_ref, ufeat, hfeat, mask,
-        deg, served, fsend, frecv, csend, crecv, msend, mrecv, rsend, rrecv, ready, meanwhile, load_feat,
+        deg, served, fsend, frecv, csend, crecv, msend, mrecv, rsend, rrecv, ready, meanwhile, load_feat, then,
     )
 
     def panel(t, k):
@@ -575,12 +591,10 @@
 
     def new_rows(t, c, v):
         p = pair_of(v, low)
-        total[...] += lax.dot_general(p, p, TN, preferred_element_type=jnp.float32)
+        pair[c] = p
         if t < ITERS - 1:
             y[c] = v
             own[t + 1, c + 1] = pair_of(v * scale_ref[c], low)
-        else:
-            pair[c] = p
 
     def solver(packed):
         gram = jnp.concatenate([packed[:, :64], packed[:, 64:]], axis=0)
@@ -596,27 +610,21 @@
 
         return solve
 
-    def first(c, _):
-        own[0, c + 1] = pair_of(y[c] * scale_ref[c], low)
-        return 0
-
-    lax.fori_loop(0, TC, first, 0, unroll=4)
     each_target(lambda k: panel(0, k).start())
     own_part(0, 1, TC - 1)
     each_source(lambda k: panel(0, k).wait_recv())
     own_part(0, 0, 1)
     own_part(0, TC - 1, TC)
-    total[...] = jnp.zeros((128, 128), jnp.float32)
-
     def rows0(c, _):
         new_rows(0, c, product(0, c))
         return 0
 
-    lax.fori_loop(0, TC, rows0, 0, unroll=8)
+    lax.fori_loop(0, TC, rows0, 0, unroll=16)
 
     solve = None
     for t in range(ITERS):
-        g = total[...]
+        p = pair[...].reshape(TC * 128, 128)
+        g = lax.dot_general(p, p, TN, preferred_element_type=jnp.float32)
         g = g[:, :64] + g[:, 64:]
         g = g[:64] + g[64:]
         packed = jnp.concatenate([g[:32], g[32:]], axis=1)
@@ -641,16 +649,14 @@
                 pair[c] = pair_of(product(t + 1, c), low)
                 return 0
 
-            lax.fori_loop(0, TC, apply, 0, unroll=8)
+            lax.fori_loop(0, TC, apply, 0, unroll=16)
         solve = solver(end_stage(t, 3))
         if more:
-            total[...] = jnp.zeros((128, 128), jnp.float32)
-
             def rows(c, _):
                 new_rows(t + 1, c, solve(pair[c]))
                 return 0
 
-            lax.fori_loop(0, TC, rows, 0, unroll=8)
+            lax.fori_loop(0, TC, rows, 0, unroll=16)
 
     factor = math.sqrt(float(NROW * 2 * NCOL * TC * PATCH))
 
@@ -662,7 +668,7 @@
             out_ref[k, c] = jnp.where(lane_low[: PATCH // 2], even, odd)
         return 0
 
-    lax.fori_loop(0, TC, last, 0, unroll=4)
+    lax.fori_loop(0, TC, last, 0, unroll=8)
 
     sent()
     for t in range(ITERS):
@@ -710,7 +716,6 @@
             pltpu.VMEM(full, jnp.float32),
             pltpu.VMEM(full, jnp.float32),
             pltpu.VMEM(full, jnp.bfloat16),
-            pltpu.VMEM((128, 128), jnp.float32),
             pltpu.VMEM((ITERS, 4, 4, 32, 128), jnp.float32),
             DMA((2, TC + 1)), DMA((2, TC + 1)), DMA((4,)), DMA((4,)), DMA((4,)), DMA((4,)),
             DMA((2, TC + 1)), DMA((2, TC + 1)),

time: 128 us -> 123 us (0.961)
  Pallas kernels: 124 us -> 119 us
    pallas_call x1, Pallas kernels: 124 us -> 119 us  [local(): pl.pallas_call(kernel, out_shape=jax.ShapeDtypeStruct((2, TC, PATCH // 2,...]
where the time goes in v6:
time: 123 us
  Pallas kernels  119 us (97%)
  local copies, waits for them, and re-layouts  3.86 us (3%)
    pallas_call x1, Pallas kernels, local(): pl.pallas_call(kernel, out_shape=jax.ShapeDtypeStruct((2, TC, PATCH // 2,...  119 us

profile of v6, /device:TPU:0, one launch (start us, length us, event | category | flops | bytes accessed | tf_op | source)
XLA Modules:
  0.0 122.7 jit_solution(14446241703617593831)
XLA Ops:
  0.0 1.9 %copy.4 = f32[4,8,32,128]{3,2,1,0:T(8,128)} copy(f32[4,8,32,128]{3,1,2,0:T(8,128)} %bitcast.7) | data formatting | bytes 1048576
  1.9 118.8 %range_finder.1 = f32[2,16,32,128]{3,2,1,0:T(8,128)} custom-call(bf16[2,16,64,1024]{3,2,1,0:T(8,128)(2,1)} %feat_hbm.1, s32[2,16,64]{2,1,0:T(8,128)} %tissue.1, f32[2,16,32,128]{3,2,1,0:T(8,128)} %bitcast.6), custom_call_target="tpu_custom_call" | custom-call | tf_op jit(solution)/shard_map/range_finder/pallas_call | solution.py:697
  120.7 1.9 %reshape.7 = f32[2,16,4096]{2,1,0:T(8,128)} reshape(f32[2,16,32,128]{3,2,1,0:T(8,128)} %range_finder.1) | data formatting | bytes 1048576 | tf_op jit(solution)/shard_map/reshape | solution.py:730

commit v7 on v6

--- a/solution.py
+++ b/solution.py
@@ -312,20 +312,6 @@
     on(0, lambda: serve(0, 2))
     on(1, lambda: serve(1, TC - 1))
 
-    near_end = (row == 0) | (row == NROW - 1)
-    late = near_end & ((col % 4 == 1) | (col % 4 == 2))
-
-    def with_sides():
-        @pl.when(jnp.logical_not(crossing))
-        def _():
-            sides()
-
-        for c in (1, TC):
-            for side in (0, 1):
-                on(side, lambda side=side, c=c: serve(side, c, c != (1, TC)[side]))
-        for c in (1, TC):
-            own_blocks(c)
-
     def arrive(g, _):
         on(0, lambda: serve(0, g + 1))
         on(1, lambda: serve(1, TC - g))
@@ -338,10 +324,6 @@
         on(0, lambda: at_home(0, g))
         on(1, lambda: at_home(1, TC + 1 - g))
 
-        @pl.when((g == 5) & jnp.logical_not(late))
-        def _():
-            with_sides()
-
         @pl.when(g < 7)
         def _():
             own_blocks(2 * g + 2)
@@ -352,9 +334,15 @@
     lax.fori_loop(2, half, arrive, 0)
     on(0, lambda: (serve(0, half + 1), at_home(0, half)))
 
-    @pl.when(late)
+    @pl.when(jnp.logical_not(crossing))
     def _():
-        with_sides()
+        sides()
+
+    for c in (1, TC):
+        for side in (0, 1):
+            on(side, lambda side=side, c=c: serve(side, c, c != (1, TC)[side]))
+    for c in (1, TC):
+        own_blocks(c)
 
     def finish(c):
         eh = jnp.concatenate([eh_ref[0, c - 1], eh_ref[1, c - 1]], axis=0).astype(jnp.float32)

time: 123 us -> 123 us (level)
  no operation moved by 1% of the time
where the time goes in v7:
time: 123 us
  Pallas kernels  119 us (97%)
  local copies, waits for them, and re-layouts  3.86 us (3%)
    pallas_call x1, Pallas kernels, local(): pl.pallas_call(kernel, out_shape=jax.ShapeDtypeStruct((2, TC, PATCH // 2,...  119 us

profile of v7, /device:TPU:0, one launch (start us, length us, event | category | flops | bytes accessed | tf_op | source)
XLA Modules:
  0.0 122.7 jit_solution(6479713348669805637)
XLA Ops:
  0.0 1.9 %copy.4 = f32[4,8,32,128]{3,2,1,0:T(8,128)} copy(f32[4,8,32,128]{3,1,2,0:T(8,128)} %bitcast.7) | data formatting | bytes 1048576
  1.9 118.8 %range_finder.1 = f32[2,16,32,128]{3,2,1,0:T(8,128)} custom-call(bf16[2,16,64,1024]{3,2,1,0:T(8,128)(2,1)} %feat_hbm.1, s32[2,16,64]{2,1,0:T(8,128)} %tissue.1, f32[2,16,32,128]{3,2,1,0:T(8,128)} %bitcast.6), custom_call_target="tpu_custom_call" | custom-call | tf_op jit(solution)/shard_map/range_finder/pallas_call | solution.py:685
  120.7 1.9 %reshape.7 = f32[2,16,4096]{2,1,0:T(8,128)} reshape(f32[2,16,32,128]{3,2,1,0:T(8,128)} %range_finder.1) | data formatting | bytes 1048576 | tf_op jit(solution)/shard_map/reshape | solution.py:718
